TPU v7x, 32 devices: a whole 2x2x4 slice. The times are simulated.
32 devices in a mesh: shard: 4 (over y, core), ctx: 8 (over z, x).
Axes of the slice: x: 2, y: 2, z: 4, core: 2. Of those that a mesh axis runs over, the one named last changes fastest.
Arguments:
- tokens: bfloat16 [16384, 576], P(('shard', 'ctx')), may hold values from -6 to 6
- cotangent: bfloat16 [16384, 576], P(('shard', 'ctx')), may hold values from -6 to 6
- seq_lengths: int32 [4, 2], P('shard'), may hold values from 1024 to 2048, as said below
- w_query: bfloat16 [2, 576, 576], P(None, 'shard'), may hold values from -0.25 to 0.25
- key_weight: bfloat16 [2, 576, 192], P(None, 'shard'), may hold values from -0.25 to 0.25
- value_weight: bfloat16 [2, 576, 192], P(None, 'shard'), may hold values from -0.25 to 0.25
- w_out: bfloat16 [2, 576, 576], P(None, 'shard'), may hold values from -3 to 3
- w_gate: bfloat16 [2, 576, 1536], P(None, 'shard'), may hold values from -0.25 to 0.25
- w_up: bfloat16 [2, 576, 1536], P(None, 'shard'), may hold values from -0.25 to 0.25
- w_down: bfloat16 [2, 1536, 576], P(None, 'shard'), may hold values from -0.15625 to 0.15625
- attn_gain: bfloat16 [2, 576], P(None, 'shard'), may hold values from 0.5 to 1.5
- ffn_gain: bfloat16 [2, 576], P(None, 'shard'), may hold values from 0.5 to 1.5
Outputs:
- output: bfloat16 [16384, 576], P(('shard', 'ctx'))
- token_grad: bfloat16 [16384, 576], P(('shard', 'ctx'))
- grad_query: float32 [2, 576, 576], P(None, 'shard')
- grad_key: float32 [2, 576, 192], P(None, 'shard')
- grad_value: float32 [2, 576, 192], P(None, 'shard')
- grad_out: float32 [2, 576, 576], P(None, 'shard')
- grad_gate: float32 [2, 576, 1536], P(None, 'shard')
- grad_up: float32 [2, 576, 1536], P(None, 'shard')
- grad_down: float32 [2, 1536, 576], P(None, 'shard')
- grad_attn_gain: float32 [2, 576], P(None, 'shard')
- grad_ffn_gain: float32 [2, 576], P(None, 'shard')
Inputs may be any that keep to these rules, and one draw needn't show every extreme that they name: `seq_lengths`: in every group the last sequence has exactly 2048 tokens; the lengths padded to multiples of 128 sum to at most 3968.
All inputs are finite; a program needn't handle non-finite values.
Results may differ from a plain program's by a relative error of at most 0.024.
Values may be sent and summed in bfloat16 or wider, within the bound.
A program may use at most 448 MiB of HBM per device.

v0:
```python
import jax
import jax.numpy as jnp
from jax import lax
from jax.sharding import PartitionSpec as P

QUERY_HEADS = 9
KEY_VALUE_HEADS = 3
HEAD_SIZE = 64
DECODER_LAYERS = 2
BLK = 128
SEQ_MOST = 4096


EPSILON = 1e-05
ROPE_BASE = 100000.0


def from_behind(value, axis, steps):
    count = lax.axis_size(axis)
    leading, last = (max(0, -steps), min(count, count - steps))
    return lax.ppermute(value, axis, [(source, source + steps) for source in range(leading, last)])


def rms_scale(value_tensor, gain_vec):
    return (
        value_tensor
        * lax.rsqrt(jnp.mean(value_tensor * value_tensor, axis=-1, keepdims=True) + EPSILON)
        * gain_vec
    )


def rotary_tables(value_tensor, token_positions):
    half_dim = value_tensor.shape[-1] // 2
    spacing = jnp.arange(half_dim, dtype=jnp.float32) * (2.0 / value_tensor.shape[-1])
    frequency = jnp.float32(ROPE_BASE) ** (-spacing)
    angles = token_positions.astype(jnp.float32)[:, None] * frequency[None, :]
    angles = jnp.concatenate([angles, angles], axis=-1)
    cosine = jnp.cos(angles)[:, None, :]
    sine_part = jnp.sin(angles)[:, None, :]
    turned = jnp.concatenate([-value_tensor[..., half_dim:], value_tensor[..., :half_dim]], axis=-1)
    return value_tensor * cosine + turned * sine_part


def row_info(row_ids, lengths, group_rows):
    padded = (lengths + BLK - 1) // BLK * BLK
    rel_ends = jnp.cumsum(padded)
    offset = group_rows - BLK - rel_ends[-1]
    seq_ends = rel_ends + offset
    starts = seq_ends - padded
    used_end = seq_ends[-1]
    inside = (row_ids[:, None] >= starts[None, :]) & (row_ids[:, None] < seq_ends[None, :])
    anywhere = jnp.any(inside, axis=1)
    numbers = jnp.arange(lengths.shape[0], dtype=jnp.int32)
    seq_ids = jnp.where(
        anywhere, jnp.sum(jnp.where(inside, numbers[None, :], 0), axis=1), lengths.shape[0]
    )
    seq_ids = jnp.where(row_ids < 0, -1, seq_ids)
    outside_first = jnp.where(row_ids < offset, 0, used_end)
    first_row = jnp.where(
        anywhere, jnp.sum(jnp.where(inside, starts[None, :], 0), axis=1), outside_first
    )
    valid = jnp.any(inside & (row_ids[:, None] < (starts + lengths)[None, :]), axis=1)
    return (seq_ids, valid, row_ids - first_row)


def outer_sum(left, right):
    return lax.dot_general(
        left, right, (((0,), (0,)), ((), ())), preferred_element_type=jnp.float32
    )


def back_dot(grad_rows, matrix):
    return lax.dot_general(
        grad_rows, matrix, (((1,), (1,)), ((), ())), preferred_element_type=jnp.float32
    )


def fetch_forward(tables, layer_no):
    return (
        lax.all_gather(tables[0][layer_no], "shard", axis=0, tiled=True),
        lax.all_gather(tables[1][layer_no], "shard", axis=0, tiled=True),
        lax.all_gather(tables[2][layer_no], "shard", axis=0, tiled=True),
        lax.all_gather(tables[3][layer_no], "shard", axis=0, tiled=True),
        lax.all_gather(tables[4][layer_no], "shard", axis=0, tiled=True),
        lax.all_gather(tables[5][layer_no], "shard", axis=0, tiled=True),
        lax.all_gather(tables[6][layer_no], "shard", axis=0, tiled=True),
        lax.all_gather(tables[7][layer_no], "shard", axis=0, tiled=True),
        lax.all_gather(tables[8][layer_no], "shard", axis=0, tiled=True),
    )


def fetch_again(tables, layer_no):
    return (
        lax.all_gather(tables[0][layer_no], "shard", axis=0, tiled=True),
        lax.all_gather(tables[1][layer_no], "shard", axis=0, tiled=True),
        lax.all_gather(tables[2][layer_no], "shard", axis=0, tiled=True),
        lax.all_gather(tables[3][layer_no], "shard", axis=0, tiled=True),
        lax.all_gather(tables[4][layer_no], "shard", axis=0, tiled=True),
        lax.all_gather(tables[5][layer_no], "shard", axis=0, tiled=True),
        lax.all_gather(tables[6][layer_no], "shard", axis=0, tiled=True),
        lax.all_gather(tables[7][layer_no], "shard", axis=0, tiled=True),
        lax.all_gather(tables[8][layer_no], "shard", axis=0, tiled=True),
    )


def collect_forward(own_pair, reach_back):
    pieces = []
    for distance in range(reach_back, 0, -1):
        pieces.append(from_behind(own_pair, "ctx", distance))
    pieces.append(own_pair)
    return jnp.concatenate(pieces, axis=0)


def collect_again(own_pair, reach_back):
    pieces = []
    for distance in range(reach_back, 0, -1):
        pieces.append(from_behind(own_pair, "ctx", distance))
    pieces.append(own_pair)
    return jnp.concatenate(pieces, axis=0)


def return_grads(window_grad, reach_back, rows_per_shard):
    totals = window_grad[reach_back * rows_per_shard :]
    for distance in range(1, reach_back + 1):
        grad_piece = window_grad[
            (reach_back - distance) * rows_per_shard : (reach_back - distance + 1) * rows_per_shard
        ]
        totals = totals + from_behind(grad_piece.astype(jnp.bfloat16), "ctx", -distance).astype(
            grad_piece.dtype
        )
    return totals


def reduce_grads(gradients):
    owned = (
        lax.psum_scatter(
            gradients[0].astype(jnp.bfloat16), "shard", scatter_dimension=0, tiled=True
        ).astype(jnp.float32),
        lax.psum_scatter(
            gradients[1].astype(jnp.bfloat16), "shard", scatter_dimension=0, tiled=True
        ).astype(jnp.float32),
        lax.psum_scatter(
            gradients[2].astype(jnp.bfloat16), "shard", scatter_dimension=0, tiled=True
        ).astype(jnp.float32),
        lax.psum_scatter(
            gradients[3].astype(jnp.bfloat16), "shard", scatter_dimension=0, tiled=True
        ).astype(jnp.float32),
        lax.psum_scatter(
            gradients[4].astype(jnp.bfloat16), "shard", scatter_dimension=0, tiled=True
        ).astype(jnp.float32),
        lax.psum_scatter(
            gradients[5].astype(jnp.bfloat16), "shard", scatter_dimension=0, tiled=True
        ).astype(jnp.float32),
        lax.psum_scatter(
            gradients[6].astype(jnp.bfloat16), "shard", scatter_dimension=0, tiled=True
        ).astype(jnp.float32),
        lax.psum_scatter(
            gradients[7].astype(jnp.bfloat16), "shard", scatter_dimension=0, tiled=True
        ).astype(jnp.float32),
        lax.psum_scatter(
            gradients[8].astype(jnp.bfloat16), "shard", scatter_dimension=0, tiled=True
        ).astype(jnp.float32),
    )
    return (
        lax.psum(owned[0].astype(jnp.bfloat16), "ctx").astype(jnp.float32),
        lax.psum(owned[1].astype(jnp.bfloat16), "ctx").astype(jnp.float32),
        lax.psum(owned[2].astype(jnp.bfloat16), "ctx").astype(jnp.float32),
        lax.psum(owned[3].astype(jnp.bfloat16), "ctx").astype(jnp.float32),
        lax.psum(owned[4].astype(jnp.bfloat16), "ctx").astype(jnp.float32),
        lax.psum(owned[5].astype(jnp.bfloat16), "ctx").astype(jnp.float32),
        lax.psum(owned[6].astype(jnp.bfloat16), "ctx").astype(jnp.float32),
        lax.psum(owned[7].astype(jnp.bfloat16), "ctx").astype(jnp.float32),
        lax.psum(owned[8].astype(jnp.bfloat16), "ctx").astype(jnp.float32),
    )


def attend_forward(window_kv, query_block, allowed_block):
    heads_per_group = QUERY_HEADS // KEY_VALUE_HEADS
    key_value_width = KEY_VALUE_HEADS * HEAD_SIZE
    score_scale = HEAD_SIZE ** (-0.5)
    block_rows = query_block.shape[0]
    outputs = []
    log_sums = []
    for head_number in range(KEY_VALUE_HEADS):
        key_rows = window_kv[:, head_number * HEAD_SIZE : (head_number + 1) * HEAD_SIZE]
        value_rows = window_kv[
            :,
            key_value_width
            + head_number * HEAD_SIZE : key_value_width
            + (head_number + 1) * HEAD_SIZE,
        ]
        queries = query_block[
            :,
            head_number
            * heads_per_group
            * HEAD_SIZE : (head_number + 1)
            * heads_per_group
            * HEAD_SIZE,
        ].reshape(block_rows, heads_per_group, HEAD_SIZE)
        scores = (
            jnp.einsum("qgd,kd->gqk", queries, key_rows, preferred_element_type=jnp.float32)
            * score_scale
        )
        scores = jnp.where(allowed_block[None], scores, -jnp.inf)
        peak_scores = jnp.max(scores, axis=-1, keepdims=True)
        raised = jnp.exp(scores - peak_scores)
        totals = jnp.sum(raised, axis=-1, keepdims=True)
        softmax_w = (raised / totals).astype(jnp.bfloat16)
        mixed_rows = jnp.einsum(
            "gqk,kd->qgd", softmax_w, value_rows, preferred_element_type=jnp.float32
        )
        outputs.append(mixed_rows.reshape(block_rows, heads_per_group * HEAD_SIZE))
        log_sums.append(jnp.transpose((peak_scores + jnp.log(totals))[..., 0]))
    return (
        jnp.concatenate(outputs, axis=1).astype(jnp.bfloat16),
        jnp.concatenate(log_sums, axis=1),
    )


def attend_backward(window_kv, running, inputs):
    query_block, allowed_block, log_sums, grad_block = inputs
    heads_per_group = QUERY_HEADS // KEY_VALUE_HEADS
    key_value_width = KEY_VALUE_HEADS * HEAD_SIZE
    score_scale = HEAD_SIZE ** (-0.5)
    block_rows = query_block.shape[0]
    grad_query_list = []
    grad_key_list = []
    grad_value_list = []
    for head_number in range(KEY_VALUE_HEADS):
        key_rows = window_kv[:, head_number * HEAD_SIZE : (head_number + 1) * HEAD_SIZE]
        value_rows = window_kv[
            :,
            key_value_width
            + head_number * HEAD_SIZE : key_value_width
            + (head_number + 1) * HEAD_SIZE,
        ]
        columns = slice(
            head_number * heads_per_group * HEAD_SIZE,
            (head_number + 1) * heads_per_group * HEAD_SIZE,
        )
        queries = query_block[:, columns].reshape(block_rows, heads_per_group, HEAD_SIZE)
        grad_heads = grad_block[:, columns].reshape(block_rows, heads_per_group, HEAD_SIZE)
        scores = (
            jnp.einsum("qgd,kd->gqk", queries, key_rows, preferred_element_type=jnp.float32)
            * score_scale
        )
        scores = jnp.where(allowed_block[None], scores, -jnp.inf)
        head_sums = jnp.transpose(
            log_sums[:, head_number * heads_per_group : (head_number + 1) * heads_per_group]
        )[..., None]
        softmax_f = jnp.exp(scores - head_sums)
        softmax_w = softmax_f.astype(jnp.bfloat16)
        grad_weights = jnp.einsum(
            "qgd,kd->gqk", grad_heads, value_rows, preferred_element_type=jnp.float32
        )
        grad_scores = softmax_f * (
            grad_weights - jnp.sum(softmax_f * grad_weights, axis=-1, keepdims=True)
        )
        low_scores = grad_scores.astype(jnp.bfloat16)
        grad_query_list.append(
            (
                jnp.einsum("gqk,kd->qgd", low_scores, key_rows, preferred_element_type=jnp.float32)
                * score_scale
            ).reshape(block_rows, heads_per_group * HEAD_SIZE)
        )
        grad_key_list.append(
            jnp.einsum("gqk,qgd->kd", low_scores, queries, preferred_element_type=jnp.float32)
            * score_scale
        )
        grad_value_list.append(
            jnp.einsum("gqk,qgd->kd", softmax_w, grad_heads, preferred_element_type=jnp.float32)
        )
    running = running + jnp.concatenate(grad_key_list + grad_value_list, axis=1)
    return (running, jnp.concatenate(grad_query_list, axis=1))


def layer_forward(residual, weights, token_positions, allowed_blocks, reach_back, blocks):
    query_mat, key_mat, value_mat, out_mat, gate_mat, up_mat, down_mat, attn_scale, ffn_scale = (
        weights
    )
    rows_per_shard = residual.shape[0]
    normed_a = rms_scale(residual, attn_scale.astype(jnp.float32)).astype(jnp.bfloat16)
    query_pre = jnp.dot(normed_a, query_mat, preferred_element_type=jnp.float32)
    key_unrotated = jnp.dot(normed_a, key_mat, preferred_element_type=jnp.float32)
    value_projected = jnp.dot(normed_a, value_mat, preferred_element_type=jnp.float32)
    queries = (
        rotary_tables(query_pre.reshape(rows_per_shard, QUERY_HEADS, HEAD_SIZE), token_positions)
        .reshape(rows_per_shard, QUERY_HEADS * HEAD_SIZE)
        .astype(jnp.bfloat16)
    )
    key_rows = (
        rotary_tables(
            key_unrotated.reshape(rows_per_shard, KEY_VALUE_HEADS, HEAD_SIZE), token_positions
        )
        .reshape(rows_per_shard, KEY_VALUE_HEADS * HEAD_SIZE)
        .astype(jnp.bfloat16)
    )
    own_pair = jnp.concatenate([key_rows, value_projected.astype(jnp.bfloat16)], axis=1)
    window_kv = collect_forward(own_pair, reach_back)
    attended, log_sums = lax.map(
        lambda inputs: attend_forward(window_kv, inputs[0], inputs[1]),
        (queries.reshape(blocks, -1, QUERY_HEADS * HEAD_SIZE), allowed_blocks),
    )
    attended = attended.reshape(rows_per_shard, QUERY_HEADS * HEAD_SIZE)
    residual_mid = residual + jnp.dot(attended, out_mat, preferred_element_type=jnp.float32)
    normed_f = rms_scale(residual_mid, ffn_scale.astype(jnp.float32)).astype(jnp.bfloat16)
    gate_act = jnp.dot(normed_f, gate_mat, preferred_element_type=jnp.float32)
    up_act = jnp.dot(normed_f, up_mat, preferred_element_type=jnp.float32)
    hidden = (jax.nn.silu(gate_act) * up_act).astype(jnp.bfloat16)
    residual_out = residual_mid + jnp.dot(hidden, down_mat, preferred_element_type=jnp.float32)
    record = (
        residual,
        normed_a,
        queries,
        attended,
        log_sums,
        residual_mid,
        normed_f,
        gate_act,
        up_act,
        hidden,
    )
    return (residual_out, record, own_pair, window_kv)


def layer_backward(
    grad_res, weights, record, window_kv, token_positions, allowed_blocks, reach_back, blocks
):
    query_mat, key_mat, value_mat, out_mat, gate_mat, up_mat, down_mat, attn_scale, ffn_scale = (
        weights
    )
    (
        residual,
        normed_a,
        queries,
        attended,
        log_sums,
        residual_mid,
        normed_f,
        gate_act,
        up_act,
        hidden,
    ) = record
    rows_per_shard = residual.shape[0]
    key_value_width = KEY_VALUE_HEADS * HEAD_SIZE
    branch_f = grad_res.astype(jnp.bfloat16)
    grad_down_mat = outer_sum(hidden, branch_f)
    grad_hidden = back_dot(branch_f, down_mat)
    sigmoid_g = jax.nn.sigmoid(gate_act)
    grad_gate_act = (
        grad_hidden * up_act * sigmoid_g * (1.0 + gate_act * (1.0 - sigmoid_g))
    ).astype(jnp.bfloat16)
    grad_up_act = (grad_hidden * gate_act * sigmoid_g).astype(jnp.bfloat16)
    grad_gate_mat = outer_sum(normed_f, grad_gate_act)
    grad_up_mat = outer_sum(normed_f, grad_up_act)
    grad_normed_f = back_dot(grad_gate_act, gate_mat) + back_dot(grad_up_act, up_mat)
    norm_value, norm_back = jax.vjp(rms_scale, residual_mid, ffn_scale.astype(jnp.float32))
    grad_mid_part, grad_ffn_scale = norm_back(grad_normed_f)
    grad_mid = grad_res + grad_mid_part
    branch_a = grad_mid.astype(jnp.bfloat16)
    grad_out_mat = outer_sum(attended, branch_a)
    grad_attended = back_dot(branch_a, out_mat).astype(jnp.bfloat16)
    window_grad, grad_queries = lax.scan(
        lambda running, inputs: attend_backward(window_kv, running, inputs),
        jnp.zeros((window_kv.shape[0], 2 * key_value_width), jnp.float32),
        (
            queries.reshape(blocks, -1, QUERY_HEADS * HEAD_SIZE),
            allowed_blocks,
            log_sums,
            grad_attended.reshape(blocks, -1, QUERY_HEADS * HEAD_SIZE),
        ),
    )
    local_gradient = return_grads(window_grad, reach_back, rows_per_shard)
    grad_query_pre = (
        rotary_tables(
            grad_queries.reshape(rows_per_shard, QUERY_HEADS, HEAD_SIZE), -token_positions
        )
        .reshape(rows_per_shard, QUERY_HEADS * HEAD_SIZE)
        .astype(jnp.bfloat16)
    )
    grad_key_pre = (
        rotary_tables(
            local_gradient[:, :key_value_width].reshape(rows_per_shard, KEY_VALUE_HEADS, HEAD_SIZE),
            -token_positions,
        )
        .reshape(rows_per_shard, key_value_width)
        .astype(jnp.bfloat16)
    )
    grad_value_pre = local_gradient[:, key_value_width:].astype(jnp.bfloat16)
    grad_query_mat = outer_sum(normed_a, grad_query_pre)
    grad_key_mat = outer_sum(normed_a, grad_key_pre)
    grad_value_mat = outer_sum(normed_a, grad_value_pre)
    grad_normed_a = (
        back_dot(grad_query_pre, query_mat)
        + back_dot(grad_key_pre, key_mat)
        + back_dot(grad_value_pre, value_mat)
    )
    norm_value, norm_back = jax.vjp(rms_scale, residual, attn_scale.astype(jnp.float32))
    grad_in_part, grad_attn_scale = norm_back(grad_normed_a)
    gradients = (
        grad_query_mat,
        grad_key_mat,
        grad_value_mat,
        grad_out_mat,
        grad_gate_mat,
        grad_up_mat,
        grad_down_mat,
        grad_attn_scale,
        grad_ffn_scale,
    )
    return (grad_mid + grad_in_part, gradients)


def body(
    tokens,
    cotangent,
    seq_lengths,
    w_query,
    key_weight,
    value_weight,
    w_out,
    w_gate,
    w_up,
    w_down,
    attn_gain,
    ffn_gain,
):
    rows_per_shard = tokens.shape[0]
    rows_per_group = rows_per_shard * lax.axis_size("ctx")
    longest = min(SEQ_MOST, rows_per_group // 2)
    reach_back = (longest - 1) // rows_per_shard + 1
    window_rows = (reach_back + 1) * rows_per_shard
    block_rows = min(512, rows_per_shard)
    blocks = rows_per_shard // block_rows
    row_ids = (lax.axis_index("ctx") - reach_back) * rows_per_shard + jnp.arange(
        window_rows, dtype=jnp.int32
    )
    key_seq, key_valid, key_pos = row_info(row_ids, seq_lengths[0], rows_per_group)
    own_ids = row_ids[reach_back * rows_per_shard :]
    own_seq = key_seq[reach_back * rows_per_shard :]
    token_positions = key_pos[reach_back * rows_per_shard :]
    allowed = (row_ids[None, :] == own_ids[:, None]) | (row_ids[None, :] <= own_ids[:, None]) & (
        key_seq[None, :] == own_seq[:, None]
    ) & key_valid[None, :]
    allowed_blocks = allowed.reshape(blocks, block_rows, window_rows)
    tables = (w_query, key_weight, value_weight, w_out, w_gate, w_up, w_down, attn_gain, ffn_gain)
    residual = tokens.astype(jnp.float32)
    saved_layers = []
    for layer_no in range(DECODER_LAYERS):
        weights = fetch_forward(tables, layer_no)
        residual, record, own_pair, window_kv = layer_forward(
            residual, weights, token_positions, allowed_blocks, reach_back, blocks
        )
        saved_layers.append((weights, record, own_pair, window_kv))
    output = residual.astype(jnp.bfloat16)
    grad_res = cotangent.astype(jnp.float32)
    reduced_layers = [None] * DECODER_LAYERS
    for layer_no in range(DECODER_LAYERS - 1, -1, -1):
        saved_weights, record, own_pair, saved_window = saved_layers[layer_no]
        weights = fetch_again(tables, layer_no)
        window_kv = collect_again(own_pair, reach_back)
        grad_res, gradients = layer_backward(
            grad_res,
            weights,
            record,
            window_kv,
            token_positions,
            allowed_blocks,
            reach_back,
            blocks,
        )
        reduced_layers[layer_no] = reduce_grads(gradients)
    token_grad = grad_res.astype(jnp.bfloat16)
    stacked = tuple(
        (
            jnp.stack(
                [reduced_layers[layer_no][member] for layer_no in range(DECODER_LAYERS)], axis=0
            )
            for member in range(9)
        )
    )
    return (output, token_grad) + stacked


def solution(mesh):
    placed = (
        P(("shard", "ctx"), None),
        P(("shard", "ctx"), None),
        P("shard", None),
        P(None, "shard", None),
        P(None, "shard", None),
        P(None, "shard", None),
        P(None, "shard", None),
        P(None, "shard", None),
        P(None, "shard", None),
        P(None, "shard", None),
        P(None, "shard"),
        P(None, "shard"),
    )
    return jax.shard_map(
        body,
        mesh=mesh,
        in_specs=placed,
        out_specs=(
            P(("shard", "ctx"), None),
            P(("shard", "ctx"), None),
            P(None, "shard", None),
            P(None, "shard", None),
            P(None, "shard", None),
            P(None, "shard", None),
            P(None, "shard", None),
            P(None, "shard", None),
            P(None, "shard", None),
            P(None, "shard"),
            P(None, "shard"),
        ),
        check_vma=False,
    )
```

profile of v0, /device:TPU:0, one launch (start us, length us, event | category | flops | bytes accessed | tf_op | source)
XLA Modules:
  0.0 1250.6 jit_solution(1326780588701102485)
XLA Ops:
  69.8 12.8 %all-gather.12 = bf16[1,576,576]{2,1,0:T(8,128)(2,1)S(1)} all-gather(bf16[1,144,576]{2,1,0:T(8,128)(2,1)S(1)} %get-tuple-element.188), channel_id=14, replica_groups=mesh['shard'=4,'ctx'=8] {'shard'}, dimensions={1}, use_global_device_ids=true | all-gather | bytes 829440 | tf_op jit(solution)/shard_map/all_gather | solution.py:80
  91.1 11.9 all-gather.3
  233.1 14.2 %collective-permute-done.4 = bf16[512,384]{0,1:T(8,128)(2,1)} collective-permute-done((bf16[512,384]{0,1:T(8,128)(2,1)}, bf16[512,384]{0,1:T(8,128)(2,1)}, u32[]{:S(2)}, u32[]{:S(2)}) %collective-permute-start.4) | collective-permute-done | bytes 393248 | tf_op jit(solution)/shard_map/ppermute | solution.py:21
  345.7 11.8 fusion.17
  381.0 14.4 %fusion.12 = (f32[3,512]{1,0:T(4,128)}, f32[2560,512,3]{1,0,2:T(8,128)}) fusion(f32[3,512,2560]{1,2,0:T(8,128)} %get-tuple-element.222, f32[3,512]{1,0:T(4,128)} %log_add_fusion.4, bf16[512,3,64]{0,2,1:T(8,128)(2,1)} %bitcast.519, bf16[2560,384]{0,1:T(8,128)(2,1)} %copy-done.37), kind=kOutput, calls=%fused_computation.22 | convolution fusion | flops 515111424 | bytes 31995904 | tf_op jit(solution)/shard_map/while/body/eval_jaxpr/qgd,kd->gqk/dot_general | solution.py:253
  395.4 11.4 fusion.14
  446.2 11.4 collective-permute-done.8
  457.6 37.2 %collective-permute-done.11 = bf16[512,384]{0,1:T(8,128)(2,1)S(1)} collective-permute-done((bf16[512,384]{0,1:T(8,128)(2,1)S(1)}, bf16[512,384]{0,1:T(8,128)(2,1)S(1)}, u32[]{:S(2)}, u32[]{:S(2)}) %collective-permute-start.11) | collective-permute-done | bytes 393248 | tf_op jit(solution)/shard_map/ppermute | solution.py:21
  523.3 11.7 fusion.8
  554.0 13.0 %fusion.3 = (f32[3,512]{1,0:T(4,128)S(1)}, f32[2560,512,3]{1,0,2:T(8,128)}) fusion(f32[3,512,2560]{1,2,0:T(8,128)} %get-tuple-element.210, f32[3,512]{1,0:T(4,128)S(1)} %copy-done.85, bf16[512,3,64]{0,2,1:T(8,128)(2,1)S(1)} %bitcast.525, bf16[2560,384]{0,1:T(8,128)(2,1)} %copy-done.36), kind=kOutput, calls=%fused_computation.7 | convolution fusion | flops 515111424 | bytes 31993856 | tf_op jit(solution)/shard_map/while/body/eval_jaxpr/qgd,kd->gqk/dot_general | solution.py:253
  615.9 13.4 %collective-permute-done.12 = bf16[512,384]{0,1:T(8,128)(2,1)S(1)} collective-permute-done((bf16[512,384]{0,1:T(8,128)(2,1)}, bf16[512,384]{0,1:T(8,128)(2,1)S(1)}, u32[]{:S(2)}, u32[]{:S(2)}) %collective-permute-start.12) | collective-permute-done | bytes 393248 | tf_op jit(solution)/shard_map/ppermute | solution.py:21
  629.3 33.1 %collective-permute-done.15 = bf16[512,384]{0,1:T(8,128)(2,1)S(1)} collective-permute-done((bf16[512,384]{0,1:T(8,128)(2,1)S(1)}, bf16[512,384]{0,1:T(8,128)(2,1)S(1)}, u32[]{:S(2)}, u32[]{:S(2)}) %collective-permute-start.15) | collective-permute-done | bytes 393248 | tf_op jit(solution)/shard_map/ppermute | solution.py:21
  734.8 19.8 %reduce-scatter.45.cloned.1.call-done = bf16[384,576]{1,0:T(8,128)(2,1)} async-done(((bf16[1536,576]{1,0:T(8,128)(2,1)}), bf16[384,576]{1,0:T(8,128)(2,1)}) %reduce-scatter.45.cloned.1.call-update) | async-done | bytes 442384
  756.6 30.8 %reduce-scatter.43.cloned.1.call-done = bf16[384,576]{1,0:T(8,128)(2,1)} async-done(((bf16[1536,576]{1,0:T(8,128)(2,1)}), bf16[384,576]{1,0:T(8,128)(2,1)}) %reduce-scatter.43.cloned.1.call-update) | async-done | bytes 442384
  789.5 23.5 %reduce-scatter.33.cloned.1.call-done = bf16[144,576]{1,0:T(8,128)(2,1)} async-done(((bf16[576,576]{1,0:T(8,128)(2,1)}), bf16[144,576]{1,0:T(8,128)(2,1)}) %reduce-scatter.33.cloned.1.call-update) | async-done | bytes 165904 | tf_op jit(solution)/shard_map/reduce_scatter | solution.py:145
  813.0 25.9 %reduce-scatter.21.cloned.1.call-done = bf16[144,576]{1,0:T(8,128)(2,1)} async-done(((bf16[576,576]{1,0:T(8,128)(2,1)}), bf16[144,576]{1,0:T(8,128)(2,1)}) %reduce-scatter.21.cloned.1.call-update) | async-done | bytes 165904 | tf_op jit(solution)/shard_map/reduce_scatter | solution.py:136
  838.9 25.3 %reduce-scatter.31.cloned.1.call-done = bf16[144,576]{1,0:T(8,128)(2,1)} async-done(((bf16[576,576]{1,0:T(8,128)(2,1)}), bf16[144,576]{1,0:T(8,128)(2,1)}) %reduce-scatter.31.cloned.1.call-update) | async-done | bytes 165904 | tf_op jit(solution)/shard_map/reduce_scatter | solution.py:145
  864.2 25.9 %reduce-scatter.19.cloned.1.call-done = bf16[144,576]{1,0:T(8,128)(2,1)} async-done(((bf16[576,576]{1,0:T(8,128)(2,1)}), bf16[144,576]{1,0:T(8,128)(2,1)}) %reduce-scatter.19.cloned.1.call-update) | async-done | bytes 165904 | tf_op jit(solution)/shard_map/reduce_scatter | solution.py:136
  890.1 32.2 %reduce-scatter.41.cloned.1.call-done = bf16[144,1536]{1,0:T(8,128)(2,1)} async-done(((bf16[576,1536]{1,0:T(8,128)(2,1)}), bf16[144,1536]{1,0:T(8,128)(2,1)}) %reduce-scatter.41.cloned.1.call-update) | async-done | bytes 442384 | tf_op jit(solution)/shard_map/reduce_scatter | solution.py:151
  922.3 32.2 %reduce-scatter.37.cloned.1.call-done = bf16[144,1536]{1,0:T(8,128)(2,1)} async-done(((bf16[576,1536]{1,0:T(8,128)(2,1)}), bf16[144,1536]{1,0:T(8,128)(2,1)}) %reduce-scatter.37.cloned.1.call-update) | async-done | bytes 442384 | tf_op jit(solution)/shard_map/reduce_scatter | solution.py:148
  954.6 31.8 %reduce-scatter.39.cloned.1.call-done = bf16[144,1536]{1,0:T(8,128)(2,1)} async-done(((bf16[576,1536]{1,0:T(8,128)(2,1)}), bf16[144,1536]{1,0:T(8,128)(2,1)}) %reduce-scatter.39.cloned.1.call-update) | async-done | bytes 442384 | tf_op jit(solution)/shard_map/reduce_scatter | solution.py:151
  986.4 32.2 %reduce-scatter.35.cloned.1.call-done = bf16[144,1536]{1,0:T(8,128)(2,1)} async-done(((bf16[576,1536]{1,0:T(8,128)(2,1)}), bf16[144,1536]{1,0:T(8,128)(2,1)}) %reduce-scatter.35.cloned.1.call-update) | async-done | bytes 442384 | tf_op jit(solution)/shard_map/reduce_scatter | solution.py:148
  1024.1 72.3 %all-reduce.15.cloned.1.call-done = (bf16[1,144,192]{2,1,0:T(8,128)(2,1)}, bf16[1,144,192]{2,1,0:T(8,128)(2,1)}, bf16[1,144,192]{2,1,0:T(8,128)(2,1)}, bf16[1,14...) async-done(((bf16[1,144,192]{2,1,0:T(8,128)(2,1)}, ...) | async-done | bytes 222352 | tf_op jit(solution)/shard_map/psum | solution.py:166
  1099.6 137.9 %all-reduce.17.cloned.1.call-done = (bf16[1,144,576]{2,1,0:T(8,128)(2,1)}, bf16[1,144,576]{2,1,0:T(8,128)(2,1)}, bf16[1,144,576]{2,1,0:T(8,128)(2,1)}, bf16[1,14...) async-done(((bf16[1,144,576]{2,1,0:T(8,128)(2,1)}, ...) | async-done | bytes 3317776 | tf_op jit(solution)/shard_map/psum | solution.py:165
  (664 shorter events, 544.9 us)
Async XLA Ops:
  7.2 191.8 %all-gather.25.cloned.1.call-start = ((), (), s32[]{:S(2)}) async-start(), calls=%async_computation.26 | async-start | bytes 2211840 | tf_op jit(solution)/shard_map/all_gather | solution.py:84
  9.5 194.2 %all-gather.27.cloned.1.call-start = ((), (), s32[]{:S(2)}) async-start(), calls=%async_computation.27 | async-start | bytes 2211840 | tf_op jit(solution)/shard_map/all_gather | solution.py:85
  10.6 199.6 %all-gather.29.cloned.1.call-start = ((), (), s32[]{:S(2)}) async-start(), calls=%async_computation.28 | async-start | bytes 2211840 | tf_op jit(solution)/shard_map/all_gather | solution.py:86
  11.7 216.1 %all-gather.35.cloned.1.call-start = ((), (), s32[]{:S(2)}) async-start(), calls=%async_computation.31 | async-start | bytes 2211840 | tf_op jit(solution)/shard_map/all_gather | solution.py:86
  12.3 307.1 %all-gather.33.cloned.1.call-start = ((), (), s32[]{:S(2)}) async-start(), calls=%async_computation.30 | async-start | bytes 2211840 | tf_op jit(solution)/shard_map/all_gather | solution.py:85
  12.9 311.2 %all-gather.31.cloned.1.call-start = ((), (), s32[]{:S(2)}) async-start(), calls=%async_computation.29 | async-start | bytes 2211840 | tf_op jit(solution)/shard_map/all_gather | solution.py:84
  47.6 80.8 %collective-permute-start.3 = (bf16[512,384]{0,1:T(8,128)(2,1)}, bf16[512,384]{0,1:T(8,128)(2,1)}, u32[]{:S(2)}, u32[]{:S(2)}) collective-permute-start(bf16[512,384]{0,1:T(8,128)(2,1)} %pad_maximum_fusion.4), channel_id=1, source_target_pairs={{0,1},{1,2},{2,3},{3,4},{4,5},{5,6},{6,7},{8,9},{9,10},{10,11},{11... | collective-permute-start | bytes 1179656 | tf_op jit(solution)/shard_map/ppermute | solution.py:21
  51.7 75.6 %collective-permute-start.2 = (bf16[512,384]{0,1:T(8,128)(2,1)}, bf16[512,384]{0,1:T(8,128)(2,1)}, u32[]{:S(2)}, u32[]{:S(2)}) collective-permute-start(bf16[512,384]{0,1:T(8,128)(2,1)} %pad_maximum_fusion.4), channel_id=1, source_target_pairs={{0,2},{1,3},{2,4},{3,5},{4,6},{5,7},{8,10},{9,11},{10,12},{11,13},... | collective-permute-start | bytes 1179656 | tf_op jit(solution)/shard_map/ppermute | solution.py:21
  55.1 71.2 %collective-permute-start.1 = (bf16[512,384]{0,1:T(8,128)(2,1)}, bf16[512,384]{0,1:T(8,128)(2,1)}, u32[]{:S(2)}, u32[]{:S(2)}) collective-permute-start(bf16[512,384]{0,1:T(8,128)(2,1)} %pad_maximum_fusion.4), channel_id=1, source_target_pairs={{0,3},{1,4},{2,5},{3,6},{4,7},{8,11},{9,12},{10,13},{11,14},{12,15... | collective-permute-start | bytes 1179656 | tf_op jit(solution)/shard_map/ppermute | solution.py:21
  61.5 673.0 %reduce-scatter.29.cloned.1.call-start = ((), (), s32[]{:S(2)}) async-start(), calls=%async_computation.19 | async-start | bytes 368640 | tf_op jit(solution)/shard_map/reduce_scatter | solution.py:142
  497.3 237.2 %reduce-scatter.25.cloned.1.call-start = ((), (), s32[]{:S(2)}) async-start(), calls=%async_computation.17 | async-start | bytes 368640 | tf_op jit(solution)/shard_map/reduce_scatter | solution.py:139
  615.8 118.7 %reduce-scatter.27.cloned.1.call-start = ((), (), s32[]{:S(2)}) async-start(), calls=%async_computation.18 | async-start | bytes 368640 | tf_op jit(solution)/shard_map/reduce_scatter | solution.py:142
  666.5 88.2 %reduce-scatter.45.cloned.1.call-start = ((), (), s32[]{:S(2)}) async-start(), calls=%async_computation.33 | async-start | bytes 2457600
  674.5 113.0 %reduce-scatter.43.cloned.1.call-start = ((), (), s32[]{:S(2)}) async-start(), calls=%async_computation.32 | async-start | bytes 2457600
  682.5 130.5 %reduce-scatter.33.cloned.1.call-start = ((), (), s32[]{:S(2)}) async-start(), calls=%async_computation.21 | async-start | bytes 921600 | tf_op jit(solution)/shard_map/reduce_scatter | solution.py:145
  684.1 154.7 %reduce-scatter.21.cloned.1.call-start = ((), (), s32[]{:S(2)}) async-start(), calls=%async_computation.15 | async-start | bytes 921600 | tf_op jit(solution)/shard_map/reduce_scatter | solution.py:136
  686.9 177.3 %reduce-scatter.31.cloned.1.call-start = ((), (), s32[]{:S(2)}) async-start(), calls=%async_computation.20 | async-start | bytes 921600 | tf_op jit(solution)/shard_map/reduce_scatter | solution.py:145
  698.3 191.8 %reduce-scatter.19.cloned.1.call-start = ((), (), s32[]{:S(2)}) async-start(), calls=%async_computation.14 | async-start | bytes 921600 | tf_op jit(solution)/shard_map/reduce_scatter | solution.py:136
  706.1 216.2 %reduce-scatter.41.cloned.1.call-start = ((), (), s32[]{:S(2)}) async-start(), calls=%async_computation.25 | async-start | bytes 2211840 | tf_op jit(solution)/shard_map/reduce_scatter | solution.py:151
  709.9 244.7 %reduce-scatter.37.cloned.1.call-start = ((), (), s32[]{:S(2)}) async-start(), calls=%async_computation.23 | async-start | bytes 2211840 | tf_op jit(solution)/shard_map/reduce_scatter | solution.py:148
  713.7 272.6 %reduce-scatter.39.cloned.1.call-start = ((), (), s32[]{:S(2)}) async-start(), calls=%async_computation.24 | async-start | bytes 2211840 | tf_op jit(solution)/shard_map/reduce_scatter | solution.py:151
  717.5 301.1 %reduce-scatter.35.cloned.1.call-start = ((), (), s32[]{:S(2)}) async-start(), calls=%async_computation.22 | async-start | bytes 2211840 | tf_op jit(solution)/shard_map/reduce_scatter | solution.py:148
  721.3 375.1 %all-reduce.15.cloned.1.call-start = ((), (), s32[]{:S(2)}) async-start(), calls=%async_computation.34 | async-start | bytes 598016 | tf_op jit(solution)/shard_map/psum | solution.py:166
  734.5 503.0 %all-reduce.17.cloned.1.call-start = ((), (), s32[]{:S(2)}) async-start(), calls=%async_computation.35 | async-start | bytes 6782976 | tf_op jit(solution)/shard_map/psum | solution.py:165
  (195 other events, 2991.9 us)
Sparse Core Ops, SparseCore 0:
  10.1 25.1 all-gather.24
  37.5 20.6 all-gather.26
  59.8 24.6 all-gather.28
  85.9 23.6 all-gather.34
  111.0 20.9 all-gather.32
  133.4 19.1 all-gather.30
  497.4 34.0 reduce-scatter.28
  615.9 40.5 reduce-scatter.24
  665.3 33.8 reduce-scatter.26
  701.4 20.1 reduce-scatter.22
  724.2 30.3 reduce-scatter.44
  757.1 30.3 reduce-scatter.42
  790.0 22.9 reduce-scatter.32
  815.9 22.9 reduce-scatter.20
  841.3 22.8 reduce-scatter.30
  867.2 22.9 reduce-scatter.18
  893.1 29.1 reduce-scatter.40
  925.4 29.1 reduce-scatter.36
  957.2 29.1 reduce-scatter.38
  989.4 29.1 reduce-scatter.34
  1024.0 72.4 all-reduce.14
  1101.4 136.1 all-reduce.16
where the time goes:
time: 1260 us; the launch traced here: 1250 us
  waiting for transfers between devices  601 us (48%)
  matrix products  317 us (25%)
  other arithmetic  143 us (11%)
  blocking collectives  85.6 us (7%)
  local copies, waits for them, and re-layouts  48.7 us (4%)
  starting transfers between devices  36.4 us (3%)
  between operations  19.3 us (2%)
    psum x1, waiting for transfers between devices, reduce_grads(): lax.psum(owned[0].astype(jnp.bfloat16), 'ctx').astype(jnp.float32)  138 us
    ppermute x16, waiting for transfers between devices, from_behind(): lax.ppermute(value, axis, [(source, source + steps) for source in range(l...  109 us
    psum x1, waiting for transfers between devices, reduce_grads(): lax.psum(owned[1].astype(jnp.bfloat16), 'ctx').astype(jnp.float32)  72.3 us
    reduce_scatter x2, waiting for transfers between devices, reduce_grads(): lax.psum_scatter(gradients[4].astype(jnp.bfloat16), 'shard', scatter_dime...  64.4 us
    reduce_scatter x2, waiting for transfers between devices, reduce_grads(): lax.psum_scatter(gradients[5].astype(jnp.bfloat16), 'shard', scatter_dime...  64 us
    convert_element_type x6, other arithmetic, attend_backward(): low_scores = grad_scores.astype(jnp.bfloat16)  61 us
    dot_general x6, matrix products, attend_backward(): jnp.einsum('qgd,kd->gqk', grad_heads, value_rows, preferred_element_type=...  60.2 us
    unnamed x24, waiting for transfers between devices  52.1 us
  transfers between devices with their start and end apart: 38, of which 17 were waited for; matrix products, arithmetic and copies ran while one was open for 30% of the time, Pallas kernels for 0%

commit v1 on v0

v1 whole, which is shorter than its diff:
```python
import jax
import jax.numpy as jnp
from jax import lax
from jax.experimental import pallas as pl
from jax.experimental.pallas import tpu as pltpu
from jax.sharding import PartitionSpec as P

QUERY_HEADS = 9
KEY_VALUE_HEADS = 3
HEAD_SIZE = 64
HEADS_PER_GROUP = QUERY_HEADS // KEY_VALUE_HEADS
QUERY_WIDTH = QUERY_HEADS * HEAD_SIZE
KV_WIDTH = KEY_VALUE_HEADS * HEAD_SIZE
GROUP_WIDTH = HEADS_PER_GROUP * HEAD_SIZE
DECODER_LAYERS = 2
BLK = 128
SEQ_MOST = 4096
CHUNK = 512
EPSILON = 1e-05
ROPE_BASE = 100000.0
LOWEST = -1e30
F32 = jnp.float32
BF16 = jnp.bfloat16


def from_behind(value, axis, steps):
    count = lax.axis_size(axis)
    leading, last = (max(0, -steps), min(count, count - steps))
    return lax.ppermute(value, axis, [(source, source + steps) for source in range(leading, last)])


def swap(value, axis, bit):
    count = lax.axis_size(axis)
    return lax.ppermute(value, axis, [(i, i ^ (1 << bit)) for i in range(count)])


def bit_count(axis):
    count = lax.axis_size(axis)
    bits = count.bit_length() - 1
    assert count == 1 << bits
    return bits


def scatter_sum(value, axis):
    index = lax.axis_index(axis)
    for bit in range(bit_count(axis)):
        value = value.reshape((value.shape[0] // 2, 2) + value.shape[1:])
        mine = (index >> bit) & 1
        kept = lax.dynamic_index_in_dim(value, mine, 1, keepdims=False)
        sent = lax.dynamic_index_in_dim(value, 1 - mine, 1, keepdims=False)
        value = (kept.astype(F32) + swap(sent, axis, bit).astype(F32)).astype(BF16)
    return value[0]


def gather_all(value, axis):
    index = lax.axis_index(axis)
    value = value[None]
    for bit in reversed(range(bit_count(axis))):
        other = swap(value, axis, bit)
        low_bit = ((index >> bit) & 1) == 0
        first = jnp.where(low_bit, value, other)
        second = jnp.where(low_bit, other, value)
        value = jnp.stack([first, second], axis=1)
        value = value.reshape((2 * value.shape[0],) + value.shape[2:])
    return value


def reduce_pack(value):
    owned = scatter_sum(value, "shard")
    flat = owned.reshape(-1)
    count = lax.axis_size("ctx")
    unit = count * 16 * 128
    size = flat.shape[0]
    padded = -(-size // unit) * unit
    if padded != size:
        flat = jnp.pad(flat, (0, padded - size))
    part = scatter_sum(flat.reshape(count, -1, 128), "ctx")
    return gather_all(part, "ctx").reshape(-1)[:size].astype(F32)


def rms_scale(value_tensor, gain_vec):
    return (
        value_tensor
        * lax.rsqrt(jnp.mean(value_tensor * value_tensor, axis=-1, keepdims=True) + EPSILON)
        * gain_vec
    )


def rotary_tables(token_positions):
    half_dim = HEAD_SIZE // 2
    spacing = jnp.arange(half_dim, dtype=F32) * (2.0 / HEAD_SIZE)
    frequency = F32(ROPE_BASE) ** (-spacing)
    angles = frequency[:, None] * token_positions.astype(F32)[None, :]
    return jnp.cos(angles), jnp.sin(angles)


def rotate(value, cosine, sine):
    rows = value.shape[1]
    halves = value.reshape(-1, 2, HEAD_SIZE // 2, rows)
    first, second = halves[:, 0], halves[:, 1]
    turned = jnp.stack(
        [first * cosine - second * sine, second * cosine + first * sine], axis=1
    )
    return turned.reshape(value.shape)


def row_limits(row_ids, lengths, group_rows):
    padded = (lengths + BLK - 1) // BLK * BLK
    rel_ends = jnp.cumsum(padded)
    offset = group_rows - BLK - rel_ends[-1]
    seq_ends = rel_ends + offset
    starts = seq_ends - padded
    used_end = seq_ends[-1]
    inside = (row_ids[:, None] >= starts[None, :]) & (row_ids[:, None] < seq_ends[None, :])
    anywhere = jnp.any(inside, axis=1)
    outside_first = jnp.where(row_ids < offset, 0, used_end)
    first_row = jnp.where(
        anywhere, jnp.sum(jnp.where(inside, starts[None, :], 0), axis=1), outside_first
    )
    valid_end = jnp.sum(jnp.where(inside, (starts + lengths)[None, :], 0), axis=1)
    key_from = jnp.where(anywhere, first_row, row_ids)
    key_to = jnp.where(anywhere, jnp.minimum(row_ids + 1, valid_end), row_ids)
    return row_ids - first_row, key_from, key_to


def contract(left, right, left_dim, right_dim):
    return lax.dot_general(
        left, right, (((left_dim,), (right_dim,)), ((), ())), preferred_element_type=F32
    )


def allowed_keys(limits_ref, chunk_start, rows):
    key_ids = lax.broadcasted_iota(jnp.int32, (CHUNK, rows), 0) + chunk_start
    return ((key_ids >= limits_ref[0:1, :]) & (key_ids < limits_ref[1:2, :])) | (
        key_ids == limits_ref[2:3, :]
    )


def attend_kernel(first_ref, query_ref, kv_ref, limits_ref, out_ref, sums_ref, total_ref):
    rows = query_ref.shape[1]
    chunks = kv_ref.shape[2] // CHUNK
    total_ref[...] = jnp.zeros_like(total_ref)

    def step(chunk, carry):
        start = pl.multiple_of(chunk * CHUNK, CHUNK)
        keys = kv_ref[0, :, pl.ds(start, CHUNK)]
        values = kv_ref[1, :, pl.ds(start, CHUNK)]
        allowed = allowed_keys(limits_ref, start, rows)
        carry = list(carry)
        for head in range(HEADS_PER_GROUP):
            cut = slice(head * HEAD_SIZE, (head + 1) * HEAD_SIZE)
            peak, summed = carry[2 * head], carry[2 * head + 1]
            scores = contract(keys, query_ref[cut, :], 0, 0)
            scores = jnp.where(allowed, scores, LOWEST)
            new_peak = jnp.maximum(peak, jnp.max(scores, axis=0, keepdims=True))
            raised = jnp.exp(scores - new_peak)
            fade = jnp.exp(peak - new_peak)
            carry[2 * head] = new_peak
            carry[2 * head + 1] = summed * fade + jnp.sum(raised, axis=0, keepdims=True)
            total_ref[cut, :] = total_ref[cut, :] * fade + contract(
                values, raised.astype(BF16), 1, 0
            )
        return tuple(carry)

    start_carry = (
        jnp.full((1, rows), LOWEST, F32),
        jnp.zeros((1, rows), F32),
    ) * HEADS_PER_GROUP
    carry = lax.fori_loop(first_ref[0], chunks, step, start_carry)
    for head in range(HEADS_PER_GROUP):
        cut = slice(head * HEAD_SIZE, (head + 1) * HEAD_SIZE)
        peak, summed = carry[2 * head], carry[2 * head + 1]
        out_ref[cut, :] = (total_ref[cut, :] / summed).astype(BF16)
        sums_ref[0, head : head + 1, :] = peak + jnp.log(summed)


def attend_back_kernel(
    first_ref,
    query_ref,
    grad_ref,
    kv_ref,
    limits_ref,
    sums_ref,
    delta_ref,
    grad_query_ref,
    grad_kv_ref,
):
    rows = query_ref.shape[1]
    chunks = kv_ref.shape[2] // CHUNK
    first = first_ref[0]
    grad_query_ref[...] = jnp.zeros_like(grad_query_ref)

    def clear(chunk, carry):
        start = pl.multiple_of(chunk * CHUNK, CHUNK)
        grad_kv_ref[:, :, pl.ds(start, CHUNK)] = jnp.zeros((2, HEAD_SIZE, CHUNK), BF16)
        return carry

    lax.fori_loop(0, first, clear, 0)

    def step(chunk, carry):
        start = pl.multiple_of(chunk * CHUNK, CHUNK)
        keys = kv_ref[0, :, pl.ds(start, CHUNK)]
        values = kv_ref[1, :, pl.ds(start, CHUNK)]
        allowed = allowed_keys(limits_ref, start, rows)
        grad_keys = jnp.zeros((HEAD_SIZE, CHUNK), F32)
        grad_values = jnp.zeros((HEAD_SIZE, CHUNK), F32)
        for head in range(HEADS_PER_GROUP):
            cut = slice(head * HEAD_SIZE, (head + 1) * HEAD_SIZE)
            query = query_ref[cut, :]
            grad = grad_ref[cut, :]
            scores = contract(keys, query, 0, 0)
            scores = jnp.where(allowed, scores, LOWEST)
            softmax = jnp.exp(scores - sums_ref[0, head : head + 1, :])
            grad_probs = contract(values, grad, 0, 0)
            grad_scores = softmax * (grad_probs - delta_ref[0, head : head + 1, :])
            low_scores = grad_scores.astype(BF16)
            grad_values += contract(grad, softmax.astype(BF16), 1, 1)
            grad_keys += contract(query, low_scores, 1, 1)
            grad_query_ref[cut, :] += contract(keys, low_scores, 1, 0)
        grad_kv_ref[0, :, pl.ds(start, CHUNK)] = grad_keys.astype(BF16)
        grad_kv_ref[1, :, pl.ds(start, CHUNK)] = grad_values.astype(BF16)
        return carry

    lax.fori_loop(first, chunks, step, 0)


def group_block(rows):
    return pl.BlockSpec((GROUP_WIDTH, rows), lambda group, first: (group, 0))


def window_block(window):
    return pl.BlockSpec((2, HEAD_SIZE, window), lambda group, first: (0, group, 0))


def stat_block(rows):
    return pl.BlockSpec((1, HEADS_PER_GROUP, rows), lambda group, first: (group, 0, 0))


def limits_block(rows):
    return pl.BlockSpec((3, rows), lambda group, first: (0, 0))


def attend(first, queries, window_kv, limits):
    rows, window = queries.shape[1], window_kv.shape[2]
    return pl.pallas_call(
        attend_kernel,
        grid_spec=pltpu.PrefetchScalarGridSpec(
            num_scalar_prefetch=1,
            grid=(KEY_VALUE_HEADS,),
            in_specs=[group_block(rows), window_block(window), limits_block(rows)],
            out_specs=[group_block(rows), stat_block(rows)],
            scratch_shapes=[pltpu.VMEM((GROUP_WIDTH, rows), F32)],
        ),
        out_shape=[
            jax.ShapeDtypeStruct((QUERY_WIDTH, rows), BF16),
            jax.ShapeDtypeStruct((KEY_VALUE_HEADS, HEADS_PER_GROUP, rows), F32),
        ],
        cost_estimate=pl.CostEstimate(
            flops=60 * QUERY_WIDTH * rows * window,
            bytes_accessed=4 * KV_WIDTH * window,
            transcendentals=QUERY_HEADS * rows * window,
        ),
        compiler_params=pltpu.CompilerParams(vmem_limit_bytes=32 << 20),
    )(first, queries, window_kv, limits)


def attend_back(first, queries, grads, window_kv, limits, sums, delta):
    rows, window = queries.shape[1], window_kv.shape[2]
    return pl.pallas_call(
        attend_back_kernel,
        grid_spec=pltpu.PrefetchScalarGridSpec(
            num_scalar_prefetch=1,
            grid=(KEY_VALUE_HEADS,),
            in_specs=[
                group_block(rows),
                group_block(rows),
                window_block(window),
                limits_block(rows),
                stat_block(rows),
                stat_block(rows),
            ],
            out_specs=[group_block(rows), window_block(window)],
        ),
        out_shape=[
            jax.ShapeDtypeStruct((QUERY_WIDTH, rows), F32),
            jax.ShapeDtypeStruct((2, KV_WIDTH, window), BF16),
        ],
        cost_estimate=pl.CostEstimate(
            flops=120 * QUERY_WIDTH * rows * window,
            bytes_accessed=8 * KV_WIDTH * window,
            transcendentals=QUERY_HEADS * rows * window,
        ),
        compiler_params=pltpu.CompilerParams(vmem_limit_bytes=32 << 20),
    )(first, queries, grads, window_kv, limits, sums, delta)


def collect_window(own_pair, reach_back):
    pieces = [from_behind(own_pair, "ctx", distance) for distance in range(reach_back, 0, -1)]
    window = jnp.concatenate(pieces + [own_pair], axis=1)
    return window.reshape(2, KV_WIDTH, -1)


def return_grads(window_grad, reach_back, rows):
    totals = window_grad[:, reach_back * rows :].astype(F32)
    for distance in range(1, reach_back + 1):
        piece = window_grad[:, (reach_back - distance) * rows : (reach_back - distance + 1) * rows]
        totals = totals + from_behind(piece, "ctx", -distance).astype(F32)
    return totals


def layer_forward(residual, weights, tables, first, limits, reach_back):
    qkv_mat, out_mat, gate_up_mat, down_mat, attn_scale, ffn_scale = weights
    cosine, sine = tables
    normed_a = rms_scale(residual, attn_scale).astype(BF16)
    projected = contract(qkv_mat, normed_a, 0, 1)
    rotated = rotate(projected[: QUERY_WIDTH + KV_WIDTH], cosine, sine)
    queries = rotated[:QUERY_WIDTH].astype(BF16) * BF16(HEAD_SIZE ** (-0.5))
    own_pair = jnp.concatenate(
        [rotated[QUERY_WIDTH:].astype(BF16), projected[QUERY_WIDTH + KV_WIDTH :].astype(BF16)],
        axis=0,
    )
    window_kv = collect_window(own_pair, reach_back)
    attended, sums = attend(first, queries, window_kv, limits)
    residual_mid = residual + contract(attended, out_mat, 0, 0)
    normed_f = rms_scale(residual_mid, ffn_scale).astype(BF16)
    gate_up = contract(normed_f, gate_up_mat, 1, 0)
    half = gate_up.shape[1] // 2
    gate_act, up_act = gate_up[:, :half], gate_up[:, half:]
    hidden = (jax.nn.silu(gate_act) * up_act).astype(BF16)
    residual_out = residual_mid + contract(hidden, down_mat, 1, 0)
    record = (
        residual,
        normed_a,
        queries,
        window_kv,
        attended,
        sums,
        residual_mid,
        normed_f,
        gate_act,
        up_act,
        hidden,
    )
    return residual_out, record


def layer_backward(grad_res, weights, record, tables, first, limits, reach_back):
    qkv_mat, out_mat, gate_up_mat, down_mat, attn_scale, ffn_scale = weights
    cosine, sine = tables
    (
        residual,
        normed_a,
        queries,
        window_kv,
        attended,
        sums,
        residual_mid,
        normed_f,
        gate_act,
        up_act,
        hidden,
    ) = record
    rows = residual.shape[0]
    shards = lax.axis_size("shard")
    branch_f = grad_res.astype(BF16)
    grad_down_mat = contract(hidden, branch_f, 0, 0).astype(BF16)
    grad_hidden = contract(branch_f, down_mat, 1, 1)
    sigmoid_g = jax.nn.sigmoid(gate_act)
    grad_gate_up = jnp.concatenate(
        [
            (grad_hidden * up_act * sigmoid_g * (1.0 + gate_act * (1.0 - sigmoid_g))).astype(BF16),
            (grad_hidden * gate_act * sigmoid_g).astype(BF16),
        ],
        axis=1,
    )
    grad_gate_up_mat = contract(normed_f, grad_gate_up, 0, 0).astype(BF16)
    reduced_gate_up = reduce_pack(grad_gate_up_mat.reshape(shards, -1, grad_gate_up.shape[1]))
    grad_normed_f = contract(grad_gate_up, gate_up_mat, 1, 1)
    _, norm_back = jax.vjp(rms_scale, residual_mid, ffn_scale)
    grad_mid_part, grad_ffn_scale = norm_back(grad_normed_f)
    grad_mid = grad_res + grad_mid_part
    branch_a = grad_mid.astype(BF16)
    grad_out_mat = contract(attended, branch_a, 1, 0).astype(BF16)
    width = branch_a.shape[1]
    reduced_down_out = reduce_pack(
        jnp.concatenate(
            [grad_down_mat.reshape(shards, -1, width), grad_out_mat.reshape(shards, -1, width)],
            axis=1,
        )
    )
    grad_attended = contract(out_mat, branch_a, 1, 1).astype(BF16)
    delta = jnp.sum(
        (grad_attended.astype(F32) * attended.astype(F32)).reshape(
            KEY_VALUE_HEADS, HEADS_PER_GROUP, HEAD_SIZE, rows
        ),
        axis=2,
    )
    grad_queries, window_grad = attend_back(
        first, queries, grad_attended, window_kv, limits, sums, delta
    )
    local_grad = return_grads(window_grad.reshape(2 * KV_WIDTH, -1), reach_back, rows)
    grad_queries = rotate(grad_queries * HEAD_SIZE ** (-0.5), cosine, -sine).astype(BF16)
    grad_keys = rotate(local_grad[:KV_WIDTH], cosine, -sine).astype(BF16)
    grad_qkv = jnp.concatenate(
        [grad_queries, grad_keys, local_grad[KV_WIDTH:].astype(BF16)], axis=0
    )
    grad_qkv_mat = contract(normed_a, grad_qkv, 0, 1).astype(BF16)
    grad_normed_a = contract(grad_qkv, qkv_mat, 0, 1)
    _, norm_back = jax.vjp(rms_scale, residual, attn_scale)
    grad_in_part, grad_attn_scale = norm_back(grad_normed_a)
    flat = jnp.concatenate(
        [
            grad_qkv_mat.reshape(shards, -1),
            grad_attn_scale.astype(BF16).reshape(shards, -1),
            grad_ffn_scale.astype(BF16).reshape(shards, -1),
        ],
        axis=1,
    )
    reduced_qkv = reduce_pack(flat)
    owned = width // shards
    hidden_width = hidden.shape[1]
    down_size = hidden_width // shards * width
    gate_up = reduced_gate_up.reshape(owned, 2 * hidden_width)
    qkv_size = owned * (QUERY_WIDTH + 2 * KV_WIDTH)
    qkv = reduced_qkv[:qkv_size].reshape(owned, -1)
    gradients = (
        qkv[:, :QUERY_WIDTH],
        qkv[:, QUERY_WIDTH : QUERY_WIDTH + KV_WIDTH],
        qkv[:, QUERY_WIDTH + KV_WIDTH :],
        reduced_down_out[down_size:].reshape(owned, width),
        gate_up[:, :hidden_width],
        gate_up[:, hidden_width:],
        reduced_down_out[:down_size].reshape(-1, width),
        reduced_qkv[qkv_size : qkv_size + owned],
        reduced_qkv[qkv_size + owned :],
    )
    return grad_mid + grad_in_part, gradients


def body(
    tokens,
    cotangent,
    seq_lengths,
    w_query,
    key_weight,
    value_weight,
    w_out,
    w_gate,
    w_up,
    w_down,
    attn_gain,
    ffn_gain,
):
    rows = tokens.shape[0]
    group_rows = rows * lax.axis_size("ctx")
    longest = min(SEQ_MOST, group_rows // 2)
    reach_back = (longest - 1) // rows + 1
    base = (lax.axis_index("ctx") - reach_back) * rows
    own_ids = lax.axis_index("ctx") * rows + jnp.arange(rows, dtype=jnp.int32)
    token_positions, key_from, key_to = row_limits(own_ids, seq_lengths[0], group_rows)
    limits = jnp.stack([key_from, key_to, own_ids], axis=0) - base
    first = jnp.clip(jnp.min(limits[0]) // CHUNK, 0, reach_back * rows // CHUNK)[None]
    tables = rotary_tables(token_positions)

    gains = gather_all(jnp.concatenate([attn_gain, ffn_gain], axis=0), "shard")
    gains = jnp.transpose(gains, (1, 0, 2)).reshape(2 * DECODER_LAYERS, -1).astype(F32)
    layer_weights = []
    for layer_no in range(DECODER_LAYERS):
        qkv_mat = gather_all(
            jnp.concatenate(
                [w_query[layer_no], key_weight[layer_no], value_weight[layer_no]], axis=1
            ),
            "shard",
        )
        out_mat = gather_all(w_out[layer_no], "shard")
        gate_up_mat = gather_all(
            jnp.concatenate([w_gate[layer_no], w_up[layer_no]], axis=1), "shard"
        )
        down_mat = gather_all(w_down[layer_no], "shard")
        layer_weights.append(
            tuple(
                matrix.reshape(-1, matrix.shape[-1])
                for matrix in (qkv_mat, out_mat, gate_up_mat, down_mat)
            )
            + (gains[layer_no], gains[DECODER_LAYERS + layer_no])
        )

    residual = tokens.astype(F32)
    records = []
    for layer_no in range(DECODER_LAYERS):
        residual, record = layer_forward(
            residual, layer_weights[layer_no], tables, first, limits, reach_back
        )
        records.append(record)
    output = residual.astype(BF16)
    grad_res = cotangent.astype(F32)
    reduced_layers = [None] * DECODER_LAYERS
    for layer_no in range(DECODER_LAYERS - 1, -1, -1):
        grad_res, reduced_layers[layer_no] = layer_backward(
            grad_res,
            layer_weights[layer_no],
            records[layer_no],
            tables,
            first,
            limits,
            reach_back,
        )
    token_grad = grad_res.astype(BF16)
    stacked = tuple(
        jnp.stack([reduced_layers[layer_no][member] for layer_no in range(DECODER_LAYERS)], axis=0)
        for member in range(9)
    )
    return (output, token_grad) + stacked


def solution(mesh):
    placed = (
        P(("shard", "ctx"), None),
        P(("shard", "ctx"), None),
        P("shard", None),
        P(None, "shard", None),
        P(None, "shard", None),
        P(None, "shard", None),
        P(None, "shard", None),
        P(None, "shard", None),
        P(None, "shard", None),
        P(None, "shard", None),
        P(None, "shard"),
        P(None, "shard"),
    )
    return jax.shard_map(
        body,
        mesh=mesh,
        in_specs=placed,
        out_specs=(
            P(("shard", "ctx"), None),
            P(("shard", "ctx"), None),
            P(None, "shard", None),
            P(None, "shard", None),
            P(None, "shard", None),
            P(None, "shard", None),
            P(None, "shard", None),
            P(None, "shard", None),
            P(None, "shard", None),
            P(None, "shard"),
            P(None, "shard"),
        ),
        check_vma=False,
    )
```

time: 1260 us -> 724 us (0.57)
  waiting for transfers between devices: 601 us -> 299 us
  matrix products: 317 us -> 48.3 us
  blocking collectives: 85.6 us -> 0 us
  starting transfers between devices: 36.4 us -> 116 us
  local copies, waits for them, and re-layouts: 48.7 us -> 119 us
  other arithmetic: 143 us -> 96.7 us
  Pallas kernels: 0 us -> 28.2 us
    dot_general x78 -> x24, matrix products: 317 us -> 48.3 us  [contract(): lax.dot_general(left, right, (((left_dim,), (right_dim,)), ((), ())), pre...]
    reduce_scatter x12 -> x0, waiting for transfers between devices: 229 us -> none  [the longest x2 64.4 us: reduce_grads(): lax.psum_scatter(gradients[4].astype(jnp.bfloat16), 'shard', scatter_dime...]
    psum x2 -> x0, waiting for transfers between devices: 210 us -> none  [the longest x1 138 us: reduce_grads(): lax.psum(owned[0].astype(jnp.bfloat16), 'ctx').astype(jnp.float32)]
    ppermute x0 -> x66, waiting for transfers between devices: none -> 161 us  [swap(): return lax.ppermute(value, axis, [(i, i ^ 1 << bit) for i in range(count)])]
    all_gather x8 -> x0, blocking collectives: 70.1 us -> none  [the longest x2 24.8 us: fetch_forward(): lax.all_gather(tables[0][layer_no], 'shard', axis=0, tiled=True)]
    unnamed x24 -> x0, waiting for transfers between devices: 52.1 us -> none
    reduce_sum x7 -> x3, other arithmetic: 45.9 us -> 1.66 us  [the longest x2 1.57 us: layer_backward(): jnp.sum((grad_attended.astype(F32) * attended.astype(F32)).reshape(KEY_VA...]
    ppermute x16, starting transfers between devices: 34.6 us -> 76.6 us  [from_behind(): lax.ppermute(value, axis, [(source, source + steps) for source in range(l...]
  transfers between devices with their start and end apart: 38 -> 82, of which waited for: 17 -> 43; matrix products, arithmetic and copies ran while one was open for 30% -> 30% of each run, Pallas kernels for 0% -> 2%
where the time goes in v1:
time: 724 us; the launch traced here: 715 us
  waiting for transfers between devices  299 us (41%)
  local copies, waits for them, and re-layouts  119 us (16%)
  starting transfers between devices  116 us (16%)
  other arithmetic  96.7 us (13%)
  matrix products  48.3 us (7%)
  Pallas kernels  28.2 us (4%)
  between operations  7.24 us (1%)
    ppermute x66, waiting for transfers between devices, swap(): return lax.ppermute(value, axis, [(i, i ^ 1 << bit) for i in range(count)])  161 us
    ppermute x16, waiting for transfers between devices, from_behind(): lax.ppermute(value, axis, [(source, source + steps) for source in range(l...  139 us
    ppermute x16, starting transfers between devices, from_behind(): lax.ppermute(value, axis, [(source, source + steps) for source in range(l...  76.6 us
    dot_general x24, matrix products, contract(): lax.dot_general(left, right, (((left_dim,), (right_dim,)), ((), ())), pre...  48.3 us
    ppermute x66, starting transfers between devices, swap(): return lax.ppermute(value, axis, [(i, i ^ 1 << bit) for i in range(count)])  39.8 us
    convert_element_type x30, other arithmetic, scatter_sum(): value = (kept.astype(F32) + swap(sent, axis, bit).astype(F32)).astype(BF16)  35.8 us
    unnamed x249, local copies, waits for them, and re-layouts  25.4 us
    concatenate x4, local copies, waits for them, and re-layouts, layer_backward(): jnp.concatenate([grad_down_mat.reshape(shards, -1, width), grad_out_mat.r...  20.3 us
  transfers between devices with their start and end apart: 82, of which 43 were waited for; matrix products, arithmetic and copies ran while one was open for 30% of the time, Pallas kernels for 2%

profile of v1, /device:TPU:0, one launch (start us, length us, event | category | flops | bytes accessed | tf_op | source)
XLA Modules:
  0.0 715.1 jit_solution(12438529368473081172)
XLA Ops:
  31.6 22.0 %collective-permute-done.14 = bf16[1,144,960]{2,1,0:T(8,128)(2,1)} collective-permute-done((bf16[1,144,960]{2,1,0:T(8,128)(2,1)}, bf16[1,144,960]{2,1,0:T(8,128)(2,1)}, u32[]{:S(2)}, u32[]{:S(2)}) %collective-permute-start.14) | collective-permute-done | bytes 276512 | tf_op jit(solution)/shard_map/ppermute | solution.py:34
  55.0 20.6 %collective-permute-done.8 = bf16[1,144,576]{2,1,0:T(8,128)(2,1)S(1)} collective-permute-done((bf16[1,144,576]{2,1,0:T(8,128)(2,1)S(1)}, bf16[1,144,576]{2,1,0:T(8,128)(2,1)S(1)}, u32[]{:S(2)}, u32[]{:S(2)}) %collective-permute-start.8) | collective-permute-done | bytes 165920 | tf_op jit(solution)/shard_map/ppermute | solution.py:34
  106.3 7.9 %collective-permute-done.6 = bf16[384,512]{1,0:T(8,128)(2,1)S(1)} collective-permute-done((bf16[384,512]{1,0:T(8,128)(2,1)S(1)}, bf16[384,512]{1,0:T(8,128)(2,1)S(1)}, u32[]{:S(2)}, u32[]{:S(2)}) %collective-permute-start.6) | collective-permute-done | bytes 393248 | tf_op jit(solution)/shard_map/ppermute | solution.py:29
  114.3 6.2 shard_map.203
  125.4 5.1 reshape_reshape.63
  135.3 5.5 reshape_reshape.59
  152.4 37.2 %collective-permute-start.16 = (bf16[384,512]{1,0:T(8,128)(2,1)S(1)}, bf16[384,512]{1,0:T(8,128)(2,1)S(1)}, u32[]{:S(2)}, u32[]{:S(2)}) collective-permute-start(bf16[384,512]{1,0:T(8,128)(2,1)S(1)} %pad_maximum_fusion.32), channel_id=1, source_target_pairs={{0,4},{1,5},{2,6},{3,7},{8,12},{9,13},{10,14},{11,15},{16,20},{17,... | collective-permute-start | bytes 1179656 | tf_op jit(solution)/shard_map/ppermute | solution.py:29
  189.7 11.0 %collective-permute-start.17 = (bf16[384,512]{1,0:T(8,128)(2,1)S(1)}, bf16[384,512]{1,0:T(8,128)(2,1)S(1)}, u32[]{:S(2)}, u32[]{:S(2)}) collective-permute-start(bf16[384,512]{1,0:T(8,128)(2,1)S(1)} %pad_maximum_fusion.32), channel_id=1, source_target_pairs={{0,3},{1,4},{2,5},{3,6},{4,7},{8,11},{9,12},{10,13},{11,14},{12,15... | collective-permute-start | bytes 1179656 | tf_op jit(solution)/shard_map/ppermute | solution.py:29
  210.2 7.5 %collective-permute-done.18 = bf16[384,512]{1,0:T(8,128)(2,1)S(1)} collective-permute-done((bf16[384,512]{1,0:T(8,128)(2,1)S(1)}, bf16[384,512]{1,0:T(8,128)(2,1)S(1)}, u32[]{:S(2)}, u32[]{:S(2)}) %collective-permute-start.18) | collective-permute-done | bytes 393248 | tf_op jit(solution)/shard_map/ppermute | solution.py:29
  217.9 6.4 shard_map.204
  244.2 7.7 %shard_map.205 = (f32[576,512]{1,0:T(8,128)S(1)}, bf16[2,192,2560]{2,1,0:T(8,128)(2,1)S(1)}) custom-call(s32[1]{0:T(128)} %bitcast.9.first_ref, bf16[576,512]{1,0:T(8,128)(2,1)S(1)} %bitcast.550, bf16[576,512]{1,0:T(8,128)(2,1)S(1)} %get-tuple-element.212.grad_ref, bf16[2,192,2560]{2,1,0:T(8,128)(2,1)S(1)} %bitcast.554, ...), custom_call_target="tpu_custom_call" | custom-call | flops 90596966400 | bytes 3932160 | tf_op jit(solution)/shard_map/pallas_call | solution.py:269
  263.2 5.2 concatenate.87
  268.4 5.2 copy.127
  282.6 23.3 %collective-permute-done.27 = bf16[384,512]{1,0:T(8,128)(2,1)} collective-permute-done((bf16[384,512]{1,0:T(8,128)(2,1)}, bf16[384,512]{1,0:T(8,128)(2,1)}, u32[]{:S(2)}, u32[]{:S(2)}) %collective-permute-start.27) | collective-permute-done | bytes 393248 | tf_op jit(solution)/shard_map/ppermute | solution.py:29
  305.9 31.2 %collective-permute-done.28 = bf16[384,512]{1,0:T(8,128)(2,1)} collective-permute-done((bf16[384,512]{1,0:T(8,128)(2,1)}, bf16[384,512]{1,0:T(8,128)(2,1)}, u32[]{:S(2)}, u32[]{:S(2)}) %collective-permute-start.28) | collective-permute-done | bytes 393248 | tf_op jit(solution)/shard_map/ppermute | solution.py:29
  337.1 32.9 %collective-permute-done.29 = bf16[384,512]{1,0:T(8,128)(2,1)} collective-permute-done((bf16[384,512]{1,0:T(8,128)(2,1)}, bf16[384,512]{1,0:T(8,128)(2,1)}, u32[]{:S(2)}, u32[]{:S(2)}) %collective-permute-start.29) | collective-permute-done | bytes 393248 | tf_op jit(solution)/shard_map/ppermute | solution.py:29
  395.3 7.9 %shard_map.206 = (f32[576,512]{1,0:T(8,128)S(1)}, bf16[2,192,2560]{2,1,0:T(8,128)(2,1)S(1)}) custom-call(s32[1]{0:T(128)} %bitcast.9.first_ref, bf16[576,512]{1,0:T(8,128)(2,1)S(1)} %bitcast.548, bf16[576,512]{1,0:T(8,128)(2,1)S(1)} %get-tuple-element.216.grad_ref, bf16[2,192,2560]{2,1,0:T(8,128)(2,1)S(1)} %bitcast.552, ...), custom_call_target="tpu_custom_call" | custom-call | flops 90596966400 | bytes 3932160 | tf_op jit(solution)/shard_map/pallas_call | solution.py:269
  422.4 5.2 copy.123
  434.4 30.7 %collective-permute-done.33 = bf16[384,512]{1,0:T(8,128)(2,1)} collective-permute-done((bf16[384,512]{1,0:T(8,128)(2,1)}, bf16[384,512]{1,0:T(8,128)(2,1)}, u32[]{:S(2)}, u32[]{:S(2)}) %collective-permute-start.33) | collective-permute-done | bytes 393248 | tf_op jit(solution)/shard_map/ppermute | solution.py:29
  480.6 14.5 %collective-permute-done.43 = bf16[1,138528]{1,0:T(2,128)(2,1)S(1)} collective-permute-done((bf16[1,138528]{1,0:T(2,128)(2,1)S(1)}, bf16[1,138528]{1,0:T(2,128)(2,1)S(1)}, u32[]{:S(2)}, u32[]{:S(2)}) %collective-permute-start.43) | collective-permute-done | bytes 277088 | tf_op jit(solution)/shard_map/ppermute | solution.py:34
  495.1 5.4 convert_reduce_fusion
  530.5 13.2 %collective-permute-done.35 = bf16[1,138528]{1,0:T(2,128)(2,1)S(1)} collective-permute-done((bf16[1,138528]{1,0:T(2,128)(2,1)S(1)}, bf16[1,138528]{1,0:T(2,128)(2,1)S(1)}, u32[]{:S(2)}, u32[]{:S(2)}) %collective-permute-start.35) | collective-permute-done | bytes 277088 | tf_op jit(solution)/shard_map/ppermute | solution.py:34
  544.3 5.2 convert_reduce_fusion.1
  703.8 5.2 collective-permute-done.73
  (708 shorter events, 385.6 us)
Async XLA Ops:
  10.7 79.0 %collective-permute-start.10 = (bf16[1,144,3072]{2,1,0:T(8,128)(2,1)}, bf16[1,144,3072]{2,1,0:T(8,128)(2,1)}, u32[]{:S(2)}, u32[]{:S(2)}) collective-permute-start(bf16[1,144,3072]{2,1,0:T(8,128)(2,1)} %maximum_bitcast_fusion.2), channel_id=1, source_target_pairs={{0,16},{8,24},{16,0},{24,8},{1,17},{9,25},{17,1},{25,9},{2,18},{10... | collective-permute-start | bytes 2654216 | tf_op jit(solution)/shard_map/ppermute | solution.py:34
  12.1 63.6 %collective-permute-start.24 = (bf16[1,384,576]{1,2,0:T(8,128)(2,1)}, bf16[1,384,576]{1,2,0:T(8,128)(2,1)}, u32[]{:S(2)}, u32[]{:S(2)}) collective-permute-start(bf16[1,384,576]{1,2,0:T(8,128)(2,1)} %slice.303), channel_id=1, source_target_pairs={{0,16},{8,24},{16,0},{24,8},{1,17},{9,25},{17,1},{25,9},{2,18},{10... | collective-permute-start | bytes 1327112 | tf_op jit(solution)/shard_map/ppermute | solution.py:34
  24.5 29.2 %collective-permute-start.14 = (bf16[1,144,960]{2,1,0:T(8,128)(2,1)}, bf16[1,144,960]{2,1,0:T(8,128)(2,1)}, u32[]{:S(2)}, u32[]{:S(2)}) collective-permute-start(bf16[1,144,960]{2,1,0:T(8,128)(2,1)} %maximum_bitcast_fusion.11), channel_id=1, source_target_pairs={{0,16},{8,24},{16,0},{24,8},{1,17},{9,25},{17,1},{25,9},{2,18},{10... | collective-permute-start | bytes 829448 | tf_op jit(solution)/shard_map/ppermute | solution.py:34
  27.3 68.4 %collective-permute-start.22 = (bf16[1,144,3072]{2,1,0:T(8,128)(2,1)}, bf16[1,144,3072]{2,1,0:T(8,128)(2,1)S(1)}, u32[]{:S(2)}, u32[]{:S(2)}) collective-permute-start(bf16[1,144,3072]{2,1,0:T(8,128)(2,1)} %maximum_bitcast_fusion.4), channel_id=1, source_target_pairs={{0,16},{8,24},{16,0},{24,8},{1,17},{9,25},{17,1},{25,9},{2,18},{10... | collective-permute-start | bytes 2654216 | tf_op jit(solution)/shard_map/ppermute | solution.py:34
  29.8 45.8 %collective-permute-start.8 = (bf16[1,144,576]{2,1,0:T(8,128)(2,1)S(1)}, bf16[1,144,576]{2,1,0:T(8,128)(2,1)S(1)}, u32[]{:S(2)}, u32[]{:S(2)}) collective-permute-start(bf16[1,144,576]{2,1,0:T(8,128)(2,1)S(1)} %get-tuple-element.164), channel_id=1, source_target_pairs={{0,16},{8,24},{16,0},{24,8},{1,17},{9,25},{17,1},{25,9},{2,18},{10... | collective-permute-start | bytes 497672 | tf_op jit(solution)/shard_map/ppermute | solution.py:34
  81.3 40.6 %collective-permute-start.25 = (bf16[2,384,576]{1,2,0:T(8,128)(2,1)S(1)}, bf16[2,384,576]{1,2,0:T(8,128)(2,1)S(1)}, u32[]{:S(2)}, u32[]{:S(2)}) collective-permute-start(bf16[2,384,576]{1,2,0:T(8,128)(2,1)S(1)} %maximum_bitcast_fusion.5), channel_id=1, source_target_pairs={{0,8},{8,0},{16,24},{24,16},{1,9},{9,1},{17,25},{25,17},{2,10},{10... | collective-permute-start | bytes 2654216 | tf_op jit(solution)/shard_map/ppermute | solution.py:34
  104.7 36.1 %collective-permute-start.11 = (bf16[2,144,3072]{2,1,0:T(8,128)(2,1)}, bf16[2,144,3072]{2,1,0:T(8,128)(2,1)}, u32[]{:S(2)}, u32[]{:S(2)}) collective-permute-start(bf16[2,144,3072]{2,1,0:T(8,128)(2,1)} %maximum_bitcast_fusion), channel_id=1, source_target_pairs={{0,8},{8,0},{16,24},{24,16},{1,9},{9,1},{17,25},{25,17},{2,10},{10... | collective-permute-start | bytes 5308424 | tf_op jit(solution)/shard_map/ppermute | solution.py:34
  114.2 91.0 %collective-permute-start.23 = (bf16[2,144,3072]{2,1,0:T(8,128)(2,1)}, bf16[2,144,3072]{2,1,0:T(8,128)(2,1)}, u32[]{:S(2)}, u32[]{:S(2)}) collective-permute-start(bf16[2,144,3072]{2,1,0:T(8,128)(2,1)} %maximum_bitcast_fusion.1), channel_id=1, source_target_pairs={{0,8},{8,0},{16,24},{24,16},{1,9},{9,1},{17,25},{25,17},{2,10},{10... | collective-permute-start | bytes 5308424 | tf_op jit(solution)/shard_map/ppermute | solution.py:34
  152.4 55.2 %collective-permute-start.16 = (bf16[384,512]{1,0:T(8,128)(2,1)S(1)}, bf16[384,512]{1,0:T(8,128)(2,1)S(1)}, u32[]{:S(2)}, u32[]{:S(2)}) collective-permute-start(bf16[384,512]{1,0:T(8,128)(2,1)S(1)} %pad_maximum_fusion.32), channel_id=1, source_target_pairs={{0,4},{1,5},{2,6},{3,7},{8,12},{9,13},{10,14},{11,15},{16,20},{17,... | collective-permute-start | bytes 1179656 | tf_op jit(solution)/shard_map/ppermute | solution.py:29
  254.2 28.4 %collective-permute-start.26 = (bf16[384,512]{1,0:T(8,128)(2,1)}, bf16[384,512]{1,0:T(8,128)(2,1)}, u32[]{:S(2)}, u32[]{:S(2)}) collective-permute-start(bf16[384,512]{1,0:T(8,128)(2,1)} %get-tuple-element.91), channel_id=1, source_target_pairs={{1,0},{2,1},{3,2},{4,3},{5,4},{6,5},{7,6},{9,8},{10,9},{11,10},{12... | collective-permute-start | bytes 1179656 | tf_op jit(solution)/shard_map/ppermute | solution.py:29
  255.5 50.4 %collective-permute-start.27 = (bf16[384,512]{1,0:T(8,128)(2,1)}, bf16[384,512]{1,0:T(8,128)(2,1)}, u32[]{:S(2)}, u32[]{:S(2)}) collective-permute-start(bf16[384,512]{1,0:T(8,128)(2,1)} %get-tuple-element.94), channel_id=1, source_target_pairs={{2,0},{3,1},{4,2},{5,3},{6,4},{7,5},{10,8},{11,9},{12,10},{13,11},... | collective-permute-start | bytes 1179656 | tf_op jit(solution)/shard_map/ppermute | solution.py:29
  256.8 80.3 %collective-permute-start.28 = (bf16[384,512]{1,0:T(8,128)(2,1)}, bf16[384,512]{1,0:T(8,128)(2,1)}, u32[]{:S(2)}, u32[]{:S(2)}) collective-permute-start(bf16[384,512]{1,0:T(8,128)(2,1)} %get-tuple-element.93), channel_id=1, source_target_pairs={{3,0},{4,1},{5,2},{6,3},{7,4},{11,8},{12,9},{13,10},{14,11},{15,12... | collective-permute-start | bytes 1179656 | tf_op jit(solution)/shard_map/ppermute | solution.py:29
  258.1 111.9 %collective-permute-start.29 = (bf16[384,512]{1,0:T(8,128)(2,1)}, bf16[384,512]{1,0:T(8,128)(2,1)}, u32[]{:S(2)}, u32[]{:S(2)}) collective-permute-start(bf16[384,512]{1,0:T(8,128)(2,1)} %get-tuple-element.92), channel_id=1, source_target_pairs={{4,0},{5,1},{6,2},{7,3},{12,8},{13,9},{14,10},{15,11},{20,16},{21,... | collective-permute-start | bytes 1179656 | tf_op jit(solution)/shard_map/ppermute | solution.py:29
  276.2 229.9 %collective-permute-start.58 = (bf16[2,528,576]{2,1,0:T(8,128)(2,1)}, bf16[2,528,576]{2,1,0:T(8,128)(2,1)}, u32[]{:S(2)}, u32[]{:S(2)}) collective-permute-start(bf16[2,528,576]{2,1,0:T(8,128)(2,1)} %fusion.9), channel_id=1, source_target_pairs={{0,8},{8,0},{16,24},{24,16},{1,9},{9,1},{17,25},{25,17},{2,10},{10... | collective-permute-start | bytes 3649544 | tf_op jit(solution)/shard_map/ppermute | solution.py:34
  405.6 28.2 %collective-permute-start.30 = (bf16[384,512]{1,0:T(8,128)(2,1)}, bf16[384,512]{1,0:T(8,128)(2,1)}, u32[]{:S(2)}, u32[]{:S(2)}) collective-permute-start(bf16[384,512]{1,0:T(8,128)(2,1)} %get-tuple-element.87), channel_id=1, source_target_pairs={{1,0},{2,1},{3,2},{4,3},{5,4},{6,5},{7,6},{9,8},{10,9},{11,10},{12... | collective-permute-start | bytes 1179656 | tf_op jit(solution)/shard_map/ppermute | solution.py:29
  409.5 55.7 %collective-permute-start.33 = (bf16[384,512]{1,0:T(8,128)(2,1)}, bf16[384,512]{1,0:T(8,128)(2,1)}, u32[]{:S(2)}, u32[]{:S(2)}) collective-permute-start(bf16[384,512]{1,0:T(8,128)(2,1)} %get-tuple-element.88), channel_id=1, source_target_pairs={{4,0},{5,1},{6,2},{7,3},{12,8},{13,9},{14,10},{15,11},{20,16},{21,... | collective-permute-start | bytes 1179656 | tf_op jit(solution)/shard_map/ppermute | solution.py:29
  433.8 130.6 %collective-permute-start.74 = (bf16[2,144,3072]{2,1,0:T(8,128)(2,1)}, bf16[2,144,3072]{2,1,0:T(8,128)(2,1)}, u32[]{:S(2)}, u32[]{:S(2)}) collective-permute-start(bf16[2,144,3072]{2,1,0:T(8,128)(2,1)} %dynamic-slice_bitcast_fusion), channel_id=1, source_target_pairs={{0,8},{8,0},{16,24},{24,16},{1,9},{9,1},{17,25},{25,17},{2,10},{10... | collective-permute-start | bytes 5308424 | tf_op jit(solution)/shard_map/ppermute | solution.py:34
  433.9 43.8 %collective-permute-start.42 = (bf16[2,138528]{1,0:T(2,128)(2,1)}, bf16[2,138528]{1,0:T(2,128)(2,1)}, u32[]{:S(2)}, u32[]{:S(2)}) collective-permute-start(bf16[2,138528]{1,0:T(2,128)(2,1)} %dynamic-slice_bitcast_fusion.2), channel_id=1, source_target_pairs={{0,8},{8,0},{16,24},{24,16},{1,9},{9,1},{17,25},{25,17},{2,10},{10... | collective-permute-start | bytes 1662344 | tf_op jit(solution)/shard_map/ppermute | solution.py:34
  434.4 93.1 %collective-permute-start.50 = (bf16[2,528,576]{2,1,0:T(8,128)(2,1)}, bf16[2,528,576]{2,1,0:T(8,128)(2,1)}, u32[]{:S(2)}, u32[]{:S(2)}) collective-permute-start(bf16[2,528,576]{2,1,0:T(8,128)(2,1)} %fusion.13), channel_id=1, source_target_pairs={{0,8},{8,0},{16,24},{24,16},{1,9},{9,1},{17,25},{25,17},{2,10},{10... | collective-permute-start | bytes 3649544 | tf_op jit(solution)/shard_map/ppermute | solution.py:34
  465.1 125.3 %collective-permute-start.66 = (bf16[2,144,3072]{2,1,0:T(8,128)(2,1)}, bf16[2,144,3072]{2,1,0:T(8,128)(2,1)}, u32[]{:S(2)}, u32[]{:S(2)}) collective-permute-start(bf16[2,144,3072]{2,1,0:T(8,128)(2,1)} %dynamic-slice_bitcast_fusion.1), channel_id=1, source_target_pairs={{0,8},{8,0},{16,24},{24,16},{1,9},{9,1},{17,25},{25,17},{2,10},{10... | collective-permute-start | bytes 5308424 | tf_op jit(solution)/shard_map/ppermute | solution.py:34
  516.0 58.8 %collective-permute-start.59 = (bf16[1,528,576]{2,1,0:T(8,128)(2,1)S(1)}, bf16[1,528,576]{2,1,0:T(8,128)(2,1)}, u32[]{:S(2)}, u32[]{:S(2)}) collective-permute-start(bf16[1,528,576]{2,1,0:T(8,128)(2,1)S(1)} %constant_dynamic-slice_fusion.5), channel_id=1, source_target_pairs={{0,16},{8,24},{16,0},{24,8},{1,17},{9,25},{17,1},{25,9},{2,18},{10... | collective-permute-start | bytes 1824776 | tf_op jit(solution)/shard_map/ppermute | solution.py:34
  543.7 53.9 %collective-permute-start.51 = (bf16[1,528,576]{2,1,0:T(8,128)(2,1)}, bf16[1,528,576]{2,1,0:T(8,128)(2,1)}, u32[]{:S(2)}, u32[]{:S(2)}) collective-permute-start(bf16[1,528,576]{2,1,0:T(8,128)(2,1)} %constant_dynamic-slice_fusion.7), channel_id=1, source_target_pairs={{0,16},{8,24},{16,0},{24,8},{1,17},{9,25},{17,1},{25,9},{2,18},{10... | collective-permute-start | bytes 1824776 | tf_op jit(solution)/shard_map/ppermute | solution.py:34
  570.6 53.6 %collective-permute-start.75 = (bf16[1,144,3072]{2,1,0:T(8,128)(2,1)}, bf16[1,144,3072]{2,1,0:T(8,128)(2,1)}, u32[]{:S(2)}, u32[]{:S(2)}) collective-permute-start(bf16[1,144,3072]{2,1,0:T(8,128)(2,1)} %constant_dynamic-slice_fusion.1), channel_id=1, source_target_pairs={{0,16},{8,24},{16,0},{24,8},{1,17},{9,25},{17,1},{25,9},{2,18},{10... | collective-permute-start | bytes 2654216 | tf_op jit(solution)/shard_map/ppermute | solution.py:34
  593.6 52.7 %collective-permute-start.67 = (bf16[1,144,3072]{2,1,0:T(8,128)(2,1)}, bf16[1,144,3072]{2,1,0:T(8,128)(2,1)}, u32[]{:S(2)}, u32[]{:S(2)}) collective-permute-start(bf16[1,144,3072]{2,1,0:T(8,128)(2,1)} %constant_dynamic-slice_fusion.3), channel_id=1, source_target_pairs={{0,16},{8,24},{16,0},{24,8},{1,17},{9,25},{17,1},{25,9},{2,18},{10... | collective-permute-start | bytes 2654216 | tf_op jit(solution)/shard_map/ppermute | solution.py:34
  (177 other events, 1564.8 us)

commit v2 on v1

--- a/solution.py
+++ b/solution.py
@@ -65,9 +65,25 @@
     return value
 
 
-def reduce_pack(value):
-    owned = scatter_sum(value, "shard")
-    flat = owned.reshape(-1)
+def after(values, event):
+    return lax.optimization_barrier((values, event))[0]
+
+
+def gather_rows(value, axis):
+    index = lax.axis_index(axis)
+    count = lax.axis_size(axis)
+    rows = value.shape[0]
+    pieces = [(0, value)]
+    for bit in reversed(range(bit_count(axis))):
+        pieces += [(away | (1 << bit), swap(piece, axis, bit)) for away, piece in pieces]
+    whole = jnp.zeros((count * rows, value.shape[1]), value.dtype)
+    for away, piece in pieces:
+        whole = lax.dynamic_update_slice(whole, piece, ((index ^ away) * rows, 0))
+    return whole
+
+
+def reduce_ctx(owned):
+    flat = jnp.concatenate([part.reshape(-1) for part in owned])
     count = lax.axis_size("ctx")
     unit = count * 16 * 128
     size = flat.shape[0]
@@ -344,7 +360,7 @@
     return residual_out, record
 
 
-def layer_backward(grad_res, weights, record, tables, first, limits, reach_back):
+def layer_backward(grad_res, weights, record, tables, first, limits, reach_back, later_owned):
     qkv_mat, out_mat, gate_up_mat, down_mat, attn_scale, ffn_scale = weights
     cosine, sine = tables
     (
@@ -374,7 +390,9 @@
         axis=1,
     )
     grad_gate_up_mat = contract(normed_f, grad_gate_up, 0, 0).astype(BF16)
-    reduced_gate_up = reduce_pack(grad_gate_up_mat.reshape(shards, -1, grad_gate_up.shape[1]))
+    owned_gate_up = scatter_sum(
+        grad_gate_up_mat.reshape(shards, -1, grad_gate_up.shape[1]), "shard"
+    )
     grad_normed_f = contract(grad_gate_up, gate_up_mat, 1, 1)
     _, norm_back = jax.vjp(rms_scale, residual_mid, ffn_scale)
     grad_mid_part, grad_ffn_scale = norm_back(grad_normed_f)
@@ -382,13 +400,12 @@
     branch_a = grad_mid.astype(BF16)
     grad_out_mat = contract(attended, branch_a, 1, 0).astype(BF16)
     width = branch_a.shape[1]
-    reduced_down_out = reduce_pack(
-        jnp.concatenate(
-            [grad_down_mat.reshape(shards, -1, width), grad_out_mat.reshape(shards, -1, width)],
-            axis=1,
-        )
-    )
+    owned_down = scatter_sum(grad_down_mat.reshape(shards, -1, width), "shard")
+    owned_out = scatter_sum(grad_out_mat.reshape(shards, -1, width), "shard")
     grad_attended = contract(out_mat, branch_a, 1, 1).astype(BF16)
+    later_reduced = [reduce_ctx(pack) for pack in later_owned]
+    if later_owned:
+        grad_attended = after(grad_attended, later_owned)
     delta = jnp.sum(
         (grad_attended.astype(F32) * attended.astype(F32)).reshape(
             KEY_VALUE_HEADS, HEADS_PER_GROUP, HEAD_SIZE, rows
@@ -399,6 +416,11 @@
         first, queries, grad_attended, window_kv, limits, sums, delta
     )
     local_grad = return_grads(window_grad.reshape(2 * KV_WIDTH, -1), reach_back, rows)
+    owned_gate_up, owned_down, owned_out, local_grad = lax.optimization_barrier(
+        (owned_gate_up, owned_down, owned_out, local_grad)
+    )
+    if later_reduced:
+        local_grad = after(local_grad, later_reduced)
     grad_queries = rotate(grad_queries * HEAD_SIZE ** (-0.5), cosine, -sine).astype(BF16)
     grad_keys = rotate(local_grad[:KV_WIDTH], cosine, -sine).astype(BF16)
     grad_qkv = jnp.concatenate(
@@ -408,22 +430,30 @@
     grad_normed_a = contract(grad_qkv, qkv_mat, 0, 1)
     _, norm_back = jax.vjp(rms_scale, residual, attn_scale)
     grad_in_part, grad_attn_scale = norm_back(grad_normed_a)
-    flat = jnp.concatenate(
+    owned_qkv = scatter_sum(grad_qkv_mat.reshape(shards, -1, grad_qkv.shape[0]), "shard")
+    scales = jnp.concatenate(
         [
-            grad_qkv_mat.reshape(shards, -1),
             grad_attn_scale.astype(BF16).reshape(shards, -1),
             grad_ffn_scale.astype(BF16).reshape(shards, -1),
         ],
         axis=1,
     )
-    reduced_qkv = reduce_pack(flat)
+    owned = [
+        [owned_gate_up],
+        [owned_down, owned_out],
+        [owned_qkv, scatter_sum(scales, "shard")],
+    ]
+    return grad_mid + grad_in_part, owned, later_reduced
+
+
+def split_gradients(reduced, shards, width, hidden_width):
+    reduced_gate_up, reduced_down_out, reduced_qkv = reduced
     owned = width // shards
-    hidden_width = hidden.shape[1]
     down_size = hidden_width // shards * width
     gate_up = reduced_gate_up.reshape(owned, 2 * hidden_width)
     qkv_size = owned * (QUERY_WIDTH + 2 * KV_WIDTH)
     qkv = reduced_qkv[:qkv_size].reshape(owned, -1)
-    gradients = (
+    return (
         qkv[:, :QUERY_WIDTH],
         qkv[:, QUERY_WIDTH : QUERY_WIDTH + KV_WIDTH],
         qkv[:, QUERY_WIDTH + KV_WIDTH :],
@@ -434,7 +464,6 @@
         reduced_qkv[qkv_size : qkv_size + owned],
         reduced_qkv[qkv_size + owned :],
     )
-    return grad_mid + grad_in_part, gradients
 
 
 def body(
@@ -465,23 +494,23 @@
     gains = gather_all(jnp.concatenate([attn_gain, ffn_gain], axis=0), "shard")
     gains = jnp.transpose(gains, (1, 0, 2)).reshape(2 * DECODER_LAYERS, -1).astype(F32)
     layer_weights = []
+    event = gains
     for layer_no in range(DECODER_LAYERS):
-        qkv_mat = gather_all(
-            jnp.concatenate(
-                [w_query[layer_no], key_weight[layer_no], value_weight[layer_no]], axis=1
-            ),
-            "shard",
+        own_qkv = jnp.concatenate(
+            [w_query[layer_no], key_weight[layer_no], value_weight[layer_no]], axis=1
         )
-        out_mat = gather_all(w_out[layer_no], "shard")
-        gate_up_mat = gather_all(
-            jnp.concatenate([w_gate[layer_no], w_up[layer_no]], axis=1), "shard"
+        if layer_no:
+            own_qkv = after(own_qkv, event)
+        qkv_mat = gather_rows(own_qkv, "shard")
+        own_out, own_gate, own_up, own_down = after(
+            (w_out[layer_no], w_gate[layer_no], w_up[layer_no], w_down[layer_no]), qkv_mat
         )
-        down_mat = gather_all(w_down[layer_no], "shard")
+        out_mat = gather_rows(own_out, "shard")
+        gate_up_mat = gather_rows(jnp.concatenate([own_gate, own_up], axis=1), "shard")
+        down_mat = gather_rows(own_down, "shard")
+        event = (gate_up_mat, down_mat)
         layer_weights.append(
-            tuple(
-                matrix.reshape(-1, matrix.shape[-1])
-                for matrix in (qkv_mat, out_mat, gate_up_mat, down_mat)
-            )
+            (qkv_mat, out_mat, gate_up_mat, down_mat)
             + (gains[layer_no], gains[DECODER_LAYERS + layer_no])
         )
 
@@ -495,8 +524,9 @@
     output = residual.astype(BF16)
     grad_res = cotangent.astype(F32)
     reduced_layers = [None] * DECODER_LAYERS
+    owned = []
     for layer_no in range(DECODER_LAYERS - 1, -1, -1):
-        grad_res, reduced_layers[layer_no] = layer_backward(
+        grad_res, owned, later_reduced = layer_backward(
             grad_res,
             layer_weights[layer_no],
             records[layer_no],
@@ -504,7 +534,15 @@
             first,
             limits,
             reach_back,
+            owned,
         )
+        if layer_no < DECODER_LAYERS - 1:
+            reduced_layers[layer_no + 1] = later_reduced
+    reduced_layers[0] = [reduce_ctx(pack) for pack in owned]
+    shards, width, hidden_width = lax.axis_size("shard"), tokens.shape[1], w_gate.shape[2]
+    reduced_layers = [
+        split_gradients(reduced, shards, width, hidden_width) for reduced in reduced_layers
+    ]
     token_grad = grad_res.astype(BF16)
     stacked = tuple(
         jnp.stack([reduced_layers[layer_no][member] for layer_no in range(DECODER_LAYERS)], axis=0)

time: 724 us -> 657 us (0.907)
  waiting for transfers between devices: 299 us -> 228 us
  starting transfers between devices: 116 us -> 168 us
  other arithmetic: 96.7 us -> 63.4 us
  local copies, waits for them, and re-layouts: 119 us -> 104 us
    ppermute x66 -> x82, waiting for transfers between devices: 161 us -> 76.1 us  [swap(): return lax.ppermute(value, axis, [(i, i ^ 1 << bit) for i in range(count)])]
    ppermute x66 -> x82, starting transfers between devices: 39.8 us -> 95.5 us  [swap(): return lax.ppermute(value, axis, [(i, i ^ 1 << bit) for i in range(count)])]
    concatenate x8 -> x2, local copies, waits for them, and re-layouts: 25.9 us -> 0.08 us  [body(): jnp.concatenate([own_gate, own_up], axis=1)]
    convert_element_type x30 -> x32, other arithmetic: 35.8 us -> 14.5 us  [scatter_sum(): value = (kept.astype(F32) + swap(sent, axis, bit).astype(F32)).astype(BF16)]
    ppermute x16, waiting for transfers between devices: 139 us -> 152 us  [from_behind(): lax.ppermute(value, axis, [(source, source + steps) for source in range(l...]
    dynamic_slice x0 -> x2, local copies, waits for them, and re-layouts: none -> 12.4 us  [scatter_sum(): kept = lax.dynamic_index_in_dim(value, mine, 1, keepdims=False)]
    another operation x54 -> x30, other arithmetic: 19.8 us -> 7.54 us  [gather_all(): value = jnp.stack([first, second], axis=1)]
    another operation x4 -> x10, local copies, waits for them, and re-layouts: 14.9 us -> 3.94 us  [the longest x2 10.6 us: body(): matrix.reshape(-1, matrix.shape[-1])]
  transfers between devices with their start and end apart: 82 -> 98, of which waited for: 43 -> 38; matrix products, arithmetic and copies ran while one was open for 30% -> 23% of each run, Pallas kernels for 2% -> 3%
where the time goes in v2:
time: 657 us; the launch traced here: 650 us
  waiting for transfers between devices  228 us (35%)
  starting transfers between devices  168 us (26%)
  local copies, waits for them, and re-layouts  104 us (16%)
  other arithmetic  63.4 us (10%)
  matrix products  50.1 us (8%)
  Pallas kernels  28.3 us (4%)
  between operations  7.21 us (1%)
    ppermute x16, waiting for transfers between devices, from_behind(): lax.ppermute(value, axis, [(source, source + steps) for source in range(l...  152 us
    ppermute x82, starting transfers between devices, swap(): return lax.ppermute(value, axis, [(i, i ^ 1 << bit) for i in range(count)])  95.5 us
    ppermute x82, waiting for transfers between devices, swap(): return lax.ppermute(value, axis, [(i, i ^ 1 << bit) for i in range(count)])  76.1 us
    ppermute x16, starting transfers between devices, from_behind(): lax.ppermute(value, axis, [(source, source + steps) for source in range(l...  72.8 us
    dot_general x24, matrix products, contract(): lax.dot_general(left, right, (((left_dim,), (right_dim,)), ((), ())), pre...  50.1 us
    unnamed x233, local copies, waits for them, and re-layouts  23.1 us
    pallas_call x2, Pallas kernels, attend_back(): pl.pallas_call(attend_back_kernel, grid_spec=pltpu.PrefetchScalarGridSpec...  15.8 us
    convert_element_type x32, other arithmetic, scatter_sum(): value = (kept.astype(F32) + swap(sent, axis, bit).astype(F32)).astype(BF16)  14.5 us
  transfers between devices with their start and end apart: 98, of which 38 were waited for; matrix products, arithmetic and copies ran while one was open for 23% of the time, Pallas kernels for 3%

profile of v2, /device:TPU:0, one launch (start us, length us, event | category | flops | bytes accessed | tf_op | source)
XLA Modules:
  0.0 649.5 jit_solution(4110445213807428427)
XLA Ops:
  48.2 6.9 %collective-permute-done.6 = bf16[384,512]{1,0:T(8,128)(2,1)S(1)} collective-permute-done((bf16[384,512]{1,0:T(8,128)(2,1)S(1)}, bf16[384,512]{1,0:T(8,128)(2,1)S(1)}, u32[]{:S(2)}, u32[]{:S(2)}) %collective-permute-start.6) | collective-permute-done | bytes 393248 | tf_op jit(solution)/shard_map/ppermute | solution.py:29
  55.7 7.4 %collective-permute-done.7 = bf16[384,512]{1,0:T(8,128)(2,1)S(1)} collective-permute-done((bf16[384,512]{1,0:T(8,128)(2,1)S(1)}, bf16[384,512]{1,0:T(8,128)(2,1)S(1)}, u32[]{:S(2)}, u32[]{:S(2)}) %collective-permute-start.7) | collective-permute-done | bytes 393248 | tf_op jit(solution)/shard_map/ppermute | solution.py:29
  63.2 6.2 shard_map.203
  70.8 5.0 collective-permute-done.12
  91.6 32.3 %collective-permute-start.21 = (bf16[384,512]{1,0:T(8,128)(2,1)S(1)}, bf16[384,512]{1,0:T(8,128)(2,1)S(1)}, u32[]{:S(2)}, u32[]{:S(2)}) collective-permute-start(bf16[384,512]{1,0:T(8,128)(2,1)S(1)} %pad_maximum_fusion.24), channel_id=1, source_target_pairs={{0,4},{1,5},{2,6},{3,7},{8,12},{9,13},{10,14},{11,15},{16,20},{17,... | collective-permute-start | bytes 1179656 | tf_op jit(solution)/shard_map/ppermute | solution.py:29
  123.9 11.1 %collective-permute-start.22 = (bf16[384,512]{1,0:T(8,128)(2,1)S(1)}, bf16[384,512]{1,0:T(8,128)(2,1)S(1)}, u32[]{:S(2)}, u32[]{:S(2)}) collective-permute-start(bf16[384,512]{1,0:T(8,128)(2,1)S(1)} %pad_maximum_fusion.24), channel_id=1, source_target_pairs={{0,3},{1,4},{2,5},{3,6},{4,7},{8,11},{9,12},{10,13},{11,14},{12,15... | collective-permute-start | bytes 1179656 | tf_op jit(solution)/shard_map/ppermute | solution.py:29
  145.6 6.5 collective-permute-done.23
  152.2 6.2 shard_map.204
  159.8 6.2 collective-permute-done.28
  188.4 8.1 %shard_map.205 = (f32[576,512]{1,0:T(8,128)S(1)}, bf16[2,192,2560]{2,1,0:T(8,128)(2,1)S(1)}) custom-call(s32[1]{0:T(128)} %bitcast.9.first_ref, bf16[576,512]{1,0:T(8,128)(2,1)S(1)} %bitcast.450, bf16[576,512]{1,0:T(8,128)(2,1)S(1)} %copy-done.6, bf16[2,192,2560]{2,1,0:T(8,128)(2,1)S(1)} %bitcast.454, s32[3,512]{1,0:T(4,128)S(1)} %add_subtract_fusion.limits_ref, ...), custom_call_target="tpu_custom_call" | custom-call | flops 90596966400 | bytes 3932160 | tf_op jit(solution)/shard_map/pallas_call | solution.py:285
  237.6 8.1 %collective-permute-start.37 = (bf16[1,384,576]{1,2,0:T(8,128)(2,1)S(1)}, bf16[1,384,576]{1,2,0:T(8,128)(2,1)S(1)}, u32[]{:S(2)}, u32[]{:S(2)}) collective-permute-start(bf16[1,384,576]{1,2,0:T(8,128)(2,1)S(1)} %constant_dynamic-slice_fusion.26), channel_id=1, source_target_pairs={{0,16},{8,24},{16,0},{24,8},{1,17},{9,25},{17,1},{25,9},{2,18},{10... | collective-permute-start | bytes 1327112 | tf_op jit(solution)/shard_map/ppermute | solution.py:34
  245.8 46.3 %collective-permute-done.42 = bf16[384,512]{1,0:T(8,128)(2,1)S(1)} collective-permute-done((bf16[384,512]{1,0:T(8,128)(2,1)S(1)}, bf16[384,512]{1,0:T(8,128)(2,1)S(1)}, u32[]{:S(2)}, u32[]{:S(2)}) %collective-permute-start.42) | collective-permute-done | bytes 393248 | tf_op jit(solution)/shard_map/ppermute | solution.py:29
  292.1 26.7 %collective-permute-done.43 = bf16[384,512]{1,0:T(8,128)(2,1)S(1)} collective-permute-done((bf16[384,512]{1,0:T(8,128)(2,1)S(1)}, bf16[384,512]{1,0:T(8,128)(2,1)S(1)}, u32[]{:S(2)}, u32[]{:S(2)}) %collective-permute-start.43) | collective-permute-done | bytes 393248 | tf_op jit(solution)/shard_map/ppermute | solution.py:29
  354.5 5.0 reshape_reshape.54
  359.5 7.6 %constant_dynamic-slice_fusion.19 = (bf16[2,1,384,576]{2,1,0,3:T(2,128)(2,1)}, bf16[2,1,384,576]{2,1,0,3:T(2,128)(2,1)}) fusion(bf16[2,2,384,576]{2,1,0,3:T(2,128)(2,1)} %reshape_reshape.54, s32[]{:T(128)S(6)} %select_n.472, s32[]{:T(128)S(6)} %select_n.473), kind=kLoop, calls=%fused_computation.327 | loop fusion | bytes 3538952 | tf_op jit(solution)/shard_map/jit(dynamic_index_in_dim)/dynamic_slice | solution.py:49
  381.0 7.7 %shard_map.206 = (f32[576,512]{1,0:T(8,128)S(1)}, bf16[2,192,2560]{2,1,0:T(8,128)(2,1)S(1)}) custom-call(s32[1]{0:T(128)} %bitcast.9.first_ref, bf16[576,512]{1,0:T(8,128)(2,1)S(1)} %bitcast.448, bf16[576,512]{1,0:T(8,128)(2,1)S(1)} %convolution_convert_fusion.8.grad_ref, bf16[2,192,2560]{2,1,0:T(8,128)(2,1)S(1)} %bitcast.452, ...), custom_call_target="tpu_custom_call" | custom-call | flops 90596966400 | bytes 3932160 | tf_op jit(solution)/shard_map/pallas_call | solution.py:285
  397.0 9.6 %collective-permute-start.92 = (bf16[4,432,128]{2,1,0:T(8,128)(2,1)S(1)}, bf16[4,432,128]{2,1,0:T(8,128)(2,1)S(1)}, u32[]{:S(2)}, u32[]{:S(2)}) collective-permute-start(bf16[4,432,128]{2,1,0:T(8,128)(2,1)S(1)} %copy-done.77), channel_id=1, source_target_pairs={{0,1},{1,0},{2,3},{3,2},{4,5},{5,4},{6,7},{7,6},{8,9},{9,8},{10,11... | collective-permute-start | bytes 1327112 | tf_op jit(solution)/shard_map/ppermute | solution.py:34
  409.2 12.0 %collective-permute-done.53 = bf16[384,512]{1,0:T(8,128)(2,1)S(1)} collective-permute-done((bf16[384,512]{1,0:T(8,128)(2,1)S(1)}, bf16[384,512]{1,0:T(8,128)(2,1)S(1)}, u32[]{:S(2)}, u32[]{:S(2)}) %collective-permute-start.53) | collective-permute-done | bytes 393248 | tf_op jit(solution)/shard_map/ppermute | solution.py:29
  421.3 11.6 %collective-permute-done.54 = bf16[384,512]{1,0:T(8,128)(2,1)S(1)} collective-permute-done((bf16[384,512]{1,0:T(8,128)(2,1)S(1)}, bf16[384,512]{1,0:T(8,128)(2,1)S(1)}, u32[]{:S(2)}, u32[]{:S(2)}) %collective-permute-start.54) | collective-permute-done | bytes 393248 | tf_op jit(solution)/shard_map/ppermute | solution.py:29
  432.9 29.2 %collective-permute-done.55 = bf16[384,512]{1,0:T(8,128)(2,1)S(1)} collective-permute-done((bf16[384,512]{1,0:T(8,128)(2,1)S(1)}, bf16[384,512]{1,0:T(8,128)(2,1)S(1)}, u32[]{:S(2)}, u32[]{:S(2)}) %collective-permute-start.55) | collective-permute-done | bytes 393248 | tf_op jit(solution)/shard_map/ppermute | solution.py:29
  463.2 7.5 %collective-permute-start.51 = (bf16[1,144,576]{2,1,0:T(8,128)(2,1)S(1)}, bf16[1,144,576]{2,1,0:T(8,128)(2,1)S(1)}, u32[]{:S(2)}, u32[]{:S(2)}) collective-permute-start(bf16[1,144,576]{2,1,0:T(8,128)(2,1)S(1)} %constant_dynamic-slice_fusion.16), channel_id=1, source_target_pairs={{0,16},{8,24},{16,0},{24,8},{1,17},{9,25},{17,1},{25,9},{2,18},{10... | collective-permute-start | bytes 497672 | tf_op jit(solution)/shard_map/ppermute | solution.py:34
  527.5 7.0 %collective-permute-done.69 = bf16[4,144,128]{2,1,0:T(8,128)(2,1)S(1)} collective-permute-done((bf16[4,144,128]{2,1,0:T(8,128)(2,1)S(1)}, bf16[4,144,128]{2,1,0:T(8,128)(2,1)S(1)}, u32[]{:S(2)}, u32[]{:S(2)}) %collective-permute-start.69) | collective-permute-done | bytes 147488 | tf_op jit(solution)/shard_map/ppermute | solution.py:34
  578.6 7.3 %collective-permute-done.86 = bf16[4,432,128]{2,1,0:T(8,128)(2,1)S(1)} collective-permute-done((bf16[4,432,128]{2,1,0:T(8,128)(2,1)S(1)}, bf16[4,432,128]{2,1,0:T(8,128)(2,1)S(1)}, u32[]{:S(2)}, u32[]{:S(2)}) %collective-permute-start.86) | collective-permute-done | bytes 442400 | tf_op jit(solution)/shard_map/ppermute | solution.py:34
  599.9 6.2 collective-permute-done.88
  (738 shorter events, 354.7 us)
Async XLA Ops:
  41.7 28.5 %collective-permute-start.15 = (bf16[384,576]{0,1:T(8,128)(2,1)S(1)}, bf16[384,576]{0,1:T(8,128)(2,1)S(1)}, u32[]{:S(2)}, u32[]{:S(2)}) collective-permute-start(bf16[384,576]{0,1:T(8,128)(2,1)S(1)} %get-tuple-element.42), channel_id=1, source_target_pairs={{0,16},{8,24},{16,0},{24,8},{1,17},{9,25},{17,1},{25,9},{2,18},{10... | collective-permute-start | bytes 1327112 | tf_op jit(solution)/shard_map/ppermute | solution.py:34
  48.1 27.7 %collective-permute-start.16 = (bf16[384,576]{0,1:T(8,128)(2,1)S(1)}, bf16[384,576]{0,1:T(8,128)(2,1)S(1)}, u32[]{:S(2)}, u32[]{:S(2)}) collective-permute-start(bf16[384,576]{0,1:T(8,128)(2,1)S(1)} %get-tuple-element.42), channel_id=1, source_target_pairs={{0,8},{8,0},{16,24},{24,16},{1,9},{9,1},{17,25},{25,17},{2,10},{10... | collective-permute-start | bytes 1327112 | tf_op jit(solution)/shard_map/ppermute | solution.py:34
  89.1 48.1 %collective-permute-start.25 = (bf16[144,576]{1,0:T(8,128)(2,1)S(1)}, bf16[144,576]{1,0:T(8,128)(2,1)S(1)}, u32[]{:S(2)}, u32[]{:S(2)}) collective-permute-start(bf16[144,576]{1,0:T(8,128)(2,1)S(1)} %get-tuple-element.45), channel_id=1, source_target_pairs={{0,16},{8,24},{16,0},{24,8},{1,17},{9,25},{17,1},{25,9},{2,18},{10... | collective-permute-start | bytes 497672 | tf_op jit(solution)/shard_map/ppermute | solution.py:34
  89.7 47.7 %collective-permute-start.26 = (bf16[144,576]{1,0:T(8,128)(2,1)S(1)}, bf16[144,576]{1,0:T(8,128)(2,1)S(1)}, u32[]{:S(2)}, u32[]{:S(2)}) collective-permute-start(bf16[144,576]{1,0:T(8,128)(2,1)S(1)} %get-tuple-element.45), channel_id=1, source_target_pairs={{0,8},{8,0},{16,24},{24,16},{1,9},{9,1},{17,25},{25,17},{2,10},{10... | collective-permute-start | bytes 497672 | tf_op jit(solution)/shard_map/ppermute | solution.py:34
  91.6 50.7 %collective-permute-start.21 = (bf16[384,512]{1,0:T(8,128)(2,1)S(1)}, bf16[384,512]{1,0:T(8,128)(2,1)S(1)}, u32[]{:S(2)}, u32[]{:S(2)}) collective-permute-start(bf16[384,512]{1,0:T(8,128)(2,1)S(1)} %pad_maximum_fusion.24), channel_id=1, source_target_pairs={{0,4},{1,5},{2,6},{3,7},{8,12},{9,13},{10,14},{11,15},{16,20},{17,... | collective-permute-start | bytes 1179656 | tf_op jit(solution)/shard_map/ppermute | solution.py:29
  135.1 24.1 %collective-permute-start.31 = (bf16[384,576]{0,1:T(8,128)(2,1)S(1)}, bf16[384,576]{0,1:T(8,128)(2,1)S(1)}, u32[]{:S(2)}, u32[]{:S(2)}) collective-permute-start(bf16[384,576]{0,1:T(8,128)(2,1)S(1)} %get-tuple-element.48), channel_id=1, source_target_pairs={{0,16},{8,24},{16,0},{24,8},{1,17},{9,25},{17,1},{25,9},{2,18},{10... | collective-permute-start | bytes 1327112 | tf_op jit(solution)/shard_map/ppermute | solution.py:34
  197.8 37.1 %collective-permute-start.40 = (bf16[384,512]{1,0:T(8,128)(2,1)}, bf16[384,512]{1,0:T(8,128)(2,1)}, u32[]{:S(2)}, u32[]{:S(2)}) collective-permute-start(bf16[384,512]{1,0:T(8,128)(2,1)} %get-tuple-element.127), channel_id=1, source_target_pairs={{1,0},{2,1},{3,2},{4,3},{5,4},{6,5},{7,6},{9,8},{10,9},{11,10},{12... | collective-permute-start | bytes 1179656 | tf_op jit(solution)/shard_map/ppermute | solution.py:29
  199.2 38.5 %collective-permute-start.41 = (bf16[384,512]{1,0:T(8,128)(2,1)}, bf16[384,512]{1,0:T(8,128)(2,1)}, u32[]{:S(2)}, u32[]{:S(2)}) collective-permute-start(bf16[384,512]{1,0:T(8,128)(2,1)} %get-tuple-element.130), channel_id=1, source_target_pairs={{2,0},{3,1},{4,2},{5,3},{6,4},{7,5},{10,8},{11,9},{12,10},{13,11},... | collective-permute-start | bytes 1179656 | tf_op jit(solution)/shard_map/ppermute | solution.py:29
  224.9 67.2 %collective-permute-start.42 = (bf16[384,512]{1,0:T(8,128)(2,1)S(1)}, bf16[384,512]{1,0:T(8,128)(2,1)S(1)}, u32[]{:S(2)}, u32[]{:S(2)}) collective-permute-start(bf16[384,512]{1,0:T(8,128)(2,1)S(1)} %copy-done.80), channel_id=1, source_target_pairs={{3,0},{4,1},{5,2},{6,3},{7,4},{11,8},{12,9},{13,10},{14,11},{15,12... | collective-permute-start | bytes 1179656 | tf_op jit(solution)/shard_map/ppermute | solution.py:29
  227.3 91.5 %collective-permute-start.43 = (bf16[384,512]{1,0:T(8,128)(2,1)S(1)}, bf16[384,512]{1,0:T(8,128)(2,1)S(1)}, u32[]{:S(2)}, u32[]{:S(2)}) collective-permute-start(bf16[384,512]{1,0:T(8,128)(2,1)S(1)} %copy-done.79), channel_id=1, source_target_pairs={{4,0},{5,1},{6,2},{7,3},{12,8},{13,9},{14,10},{15,11},{20,16},{21,... | collective-permute-start | bytes 1179656 | tf_op jit(solution)/shard_map/ppermute | solution.py:29
  233.3 88.5 %collective-permute-start.35 = (bf16[1,144,3072]{2,1,0:T(8,128)(2,1)S(1)}, bf16[1,144,3072]{2,1,0:T(8,128)(2,1)S(1)}, u32[]{:S(2)}, u32[]{:S(2)}) collective-permute-start(bf16[1,144,3072]{2,1,0:T(8,128)(2,1)S(1)} %constant_dynamic-slice_fusion.29), channel_id=1, source_target_pairs={{0,16},{8,24},{16,0},{24,8},{1,17},{9,25},{17,1},{25,9},{2,18},{10... | collective-permute-start | bytes 2654216 | tf_op jit(solution)/shard_map/ppermute | solution.py:34
  234.9 85.2 %collective-permute-start.39 = (bf16[1,144,576]{2,1,0:T(8,128)(2,1)S(1)}, bf16[1,144,576]{2,1,0:T(8,128)(2,1)S(1)}, u32[]{:S(2)}, u32[]{:S(2)}) collective-permute-start(bf16[1,144,576]{2,1,0:T(8,128)(2,1)S(1)} %constant_dynamic-slice_fusion.25), channel_id=1, source_target_pairs={{0,16},{8,24},{16,0},{24,8},{1,17},{9,25},{17,1},{25,9},{2,18},{10... | collective-permute-start | bytes 497672 | tf_op jit(solution)/shard_map/ppermute | solution.py:34
  237.6 83.2 %collective-permute-start.37 = (bf16[1,384,576]{1,2,0:T(8,128)(2,1)S(1)}, bf16[1,384,576]{1,2,0:T(8,128)(2,1)S(1)}, u32[]{:S(2)}, u32[]{:S(2)}) collective-permute-start(bf16[1,384,576]{1,2,0:T(8,128)(2,1)S(1)} %constant_dynamic-slice_fusion.26), channel_id=1, source_target_pairs={{0,16},{8,24},{16,0},{24,8},{1,17},{9,25},{17,1},{25,9},{2,18},{10... | collective-permute-start | bytes 1327112 | tf_op jit(solution)/shard_map/ppermute | solution.py:34
  343.7 27.6 %collective-permute-start.44 = (bf16[2,288]{1,0:T(2,128)(2,1)S(1)}, bf16[2,288]{1,0:T(2,128)(2,1)S(1)}, u32[]{:S(2)}, u32[]{:S(2)}) collective-permute-start(bf16[2,288]{1,0:T(2,128)(2,1)S(1)} %bitcast.526), channel_id=1, source_target_pairs={{0,8},{8,0},{16,24},{24,16},{1,9},{9,1},{17,25},{25,17},{2,10},{10... | collective-permute-start | bytes 3464 | tf_op jit(solution)/shard_map/ppermute | solution.py:34
  354.5 39.6 %collective-permute-start.56 = (bf16[4,304,128]{2,1,0:T(8,128)(2,1)}, bf16[4,304,128]{2,1,0:T(8,128)(2,1)}, u32[]{:S(2)}, u32[]{:S(2)}) collective-permute-start(bf16[4,304,128]{2,1,0:T(8,128)(2,1)} %dynamic-slice_bitcast_fusion.9), channel_id=1, source_target_pairs={{0,1},{1,0},{2,3},{3,2},{4,5},{5,4},{6,7},{7,6},{8,9},{9,8},{10,11... | collective-permute-start | bytes 933896 | tf_op jit(solution)/shard_map/ppermute | solution.py:34
  369.2 27.7 %collective-permute-start.50 = (bf16[2,144,576]{2,1,0:T(8,128)(2,1)}, bf16[2,144,576]{2,1,0:T(8,128)(2,1)}, u32[]{:S(2)}, u32[]{:S(2)}) collective-permute-start(bf16[2,144,576]{2,1,0:T(8,128)(2,1)} %dynamic-slice_bitcast_fusion.6), channel_id=1, source_target_pairs={{0,8},{8,0},{16,24},{24,16},{1,9},{9,1},{17,25},{25,17},{2,10},{10... | collective-permute-start | bytes 995336 | tf_op jit(solution)/shard_map/ppermute | solution.py:34
  390.4 30.8 %collective-permute-start.53 = (bf16[384,512]{1,0:T(8,128)(2,1)S(1)}, bf16[384,512]{1,0:T(8,128)(2,1)S(1)}, u32[]{:S(2)}, u32[]{:S(2)}) collective-permute-start(bf16[384,512]{1,0:T(8,128)(2,1)S(1)} %get-tuple-element.126), channel_id=1, source_target_pairs={{2,0},{3,1},{4,2},{5,3},{6,4},{7,5},{10,8},{11,9},{12,10},{13,11},... | collective-permute-start | bytes 1179656 | tf_op jit(solution)/shard_map/ppermute | solution.py:29
  391.7 41.1 %collective-permute-start.54 = (bf16[384,512]{1,0:T(8,128)(2,1)S(1)}, bf16[384,512]{1,0:T(8,128)(2,1)S(1)}, u32[]{:S(2)}, u32[]{:S(2)}) collective-permute-start(bf16[384,512]{1,0:T(8,128)(2,1)S(1)} %get-tuple-element.125), channel_id=1, source_target_pairs={{3,0},{4,1},{5,2},{6,3},{7,4},{11,8},{12,9},{13,10},{14,11},{15,12... | collective-permute-start | bytes 1179656 | tf_op jit(solution)/shard_map/ppermute | solution.py:29
  394.1 67.9 %collective-permute-start.55 = (bf16[384,512]{1,0:T(8,128)(2,1)S(1)}, bf16[384,512]{1,0:T(8,128)(2,1)S(1)}, u32[]{:S(2)}, u32[]{:S(2)}) collective-permute-start(bf16[384,512]{1,0:T(8,128)(2,1)S(1)} %get-tuple-element.124), channel_id=1, source_target_pairs={{4,0},{5,1},{6,2},{7,3},{12,8},{13,9},{14,10},{15,11},{20,16},{21,... | collective-permute-start | bytes 1179656 | tf_op jit(solution)/shard_map/ppermute | solution.py:29
  397.0 66.3 %collective-permute-start.92 = (bf16[4,432,128]{2,1,0:T(8,128)(2,1)S(1)}, bf16[4,432,128]{2,1,0:T(8,128)(2,1)S(1)}, u32[]{:S(2)}, u32[]{:S(2)}) collective-permute-start(bf16[4,432,128]{2,1,0:T(8,128)(2,1)S(1)} %copy-done.77), channel_id=1, source_target_pairs={{0,1},{1,0},{2,3},{3,2},{4,5},{5,4},{6,7},{7,6},{8,9},{9,8},{10,11... | collective-permute-start | bytes 1327112 | tf_op jit(solution)/shard_map/ppermute | solution.py:34
  409.2 72.1 %collective-permute-start.62 = (bf16[2,144,960]{2,1,0:T(8,128)(2,1)S(1)}, bf16[2,144,960]{2,1,0:T(8,128)(2,1)S(1)}, u32[]{:S(2)}, u32[]{:S(2)}) collective-permute-start(bf16[2,144,960]{2,1,0:T(8,128)(2,1)S(1)} %copy-done.72), channel_id=1, source_target_pairs={{0,8},{8,0},{16,24},{24,16},{1,9},{9,1},{17,25},{25,17},{2,10},{10... | collective-permute-start | bytes 1658888 | tf_op jit(solution)/shard_map/ppermute | solution.py:34
  421.3 85.1 %collective-permute-start.48 = (bf16[2,384,576]{1,2,0:T(8,128)(2,1)}, bf16[2,384,576]{1,2,0:T(8,128)(2,1)}, u32[]{:S(2)}, u32[]{:S(2)}) collective-permute-start(bf16[2,384,576]{1,2,0:T(8,128)(2,1)} %bitcast.439), channel_id=1, source_target_pairs={{0,8},{8,0},{16,24},{24,16},{1,9},{9,1},{17,25},{25,17},{2,10},{10... | collective-permute-start | bytes 2654216 | tf_op jit(solution)/shard_map/ppermute | solution.py:34
  432.9 103.6 %collective-permute-start.46 = (bf16[2,144,3072]{2,1,0:T(8,128)(2,1)}, bf16[2,144,3072]{2,1,0:T(8,128)(2,1)}, u32[]{:S(2)}, u32[]{:S(2)}) collective-permute-start(bf16[2,144,3072]{2,1,0:T(8,128)(2,1)} %dynamic-slice_bitcast_fusion), channel_id=1, source_target_pairs={{0,8},{8,0},{16,24},{24,16},{1,9},{9,1},{17,25},{25,17},{2,10},{10... | collective-permute-start | bytes 5308424 | tf_op jit(solution)/shard_map/ppermute | solution.py:34
  562.5 31.7 %collective-permute-start.70 = (bf16[2,144,960]{2,1,0:T(8,128)(2,1)}, bf16[2,144,960]{2,1,0:T(8,128)(2,1)}, u32[]{:S(2)}, u32[]{:S(2)}) collective-permute-start(bf16[2,144,960]{2,1,0:T(8,128)(2,1)} %dynamic-slice_bitcast_fusion.2), channel_id=1, source_target_pairs={{0,8},{8,0},{16,24},{24,16},{1,9},{9,1},{17,25},{25,17},{2,10},{10... | collective-permute-start | bytes 1658888 | tf_op jit(solution)/shard_map/ppermute | solution.py:34
  (185 other events, 1697.8 us)

commit v3 on v2

--- a/solution.py
+++ b/solution.py
@@ -403,7 +403,7 @@
     owned_down = scatter_sum(grad_down_mat.reshape(shards, -1, width), "shard")
     owned_out = scatter_sum(grad_out_mat.reshape(shards, -1, width), "shard")
     grad_attended = contract(out_mat, branch_a, 1, 1).astype(BF16)
-    later_reduced = [reduce_ctx(pack) for pack in later_owned]
+    later_reduced = [reduce_ctx(pack) for pack in later_owned[:2]]
     if later_owned:
         grad_attended = after(grad_attended, later_owned)
     delta = jnp.sum(
@@ -524,7 +524,7 @@
     output = residual.astype(BF16)
     grad_res = cotangent.astype(F32)
     reduced_layers = [None] * DECODER_LAYERS
-    owned = []
+    owned, qkv_packs = [], []
     for layer_no in range(DECODER_LAYERS - 1, -1, -1):
         grad_res, owned, later_reduced = layer_backward(
             grad_res,
@@ -536,9 +536,14 @@
             reach_back,
             owned,
         )
+        qkv_packs += owned[2]
         if layer_no < DECODER_LAYERS - 1:
             reduced_layers[layer_no + 1] = later_reduced
-    reduced_layers[0] = [reduce_ctx(pack) for pack in owned]
+    reduced_layers[0] = [reduce_ctx(pack) for pack in owned[:2]]
+    both_qkv = jnp.split(reduce_ctx(qkv_packs), DECODER_LAYERS)
+    reduced_layers = [
+        reduced + [qkv] for reduced, qkv in zip(reduced_layers, reversed(both_qkv))
+    ]
     shards, width, hidden_width = lax.axis_size("shard"), tokens.shape[1], w_gate.shape[2]
     reduced_layers = [
         split_gradients(reduced, shards, width, hidden_width) for reduced in reduced_layers

time: 657 us -> 642 us (0.977)
  starting transfers between devices: 168 us -> 141 us
  waiting for transfers between devices: 228 us -> 243 us
    ppermute x82 -> x76, starting transfers between devices: 95.5 us -> 68.2 us  [swap(): return lax.ppermute(value, axis, [(i, i ^ 1 << bit) for i in range(count)])]
    ppermute x16, waiting for transfers between devices: 152 us -> 167 us  [from_behind(): lax.ppermute(value, axis, [(source, source + steps) for source in range(l...]
    convert_element_type x32 -> x29, other arithmetic: 14.5 us -> 15.3 us  [scatter_sum(): value = (kept.astype(F32) + swap(sent, axis, bit).astype(F32)).astype(BF16)]
    unnamed x233 -> x223, local copies, waits for them, and re-layouts: 23.1 us -> 22.8 us
    ppermute x82 -> x76, waiting for transfers between devices: 76.1 us -> 76.4 us  [swap(): return lax.ppermute(value, axis, [(i, i ^ 1 << bit) for i in range(count)])]
    squeeze x34 -> x31, local copies, waits for them, and re-layouts: 14.3 us -> 14.1 us  [scatter_sum(): sent = lax.dynamic_index_in_dim(value, 1 - mine, 1, keepdims=False)]
  transfers between devices with their start and end apart: 98 -> 92, of which waited for: 38 -> 42; matrix products, arithmetic and copies ran while one was open for 23% -> 23% of each run, Pallas kernels for 3% -> 3%
where the time goes in v3:
time: 642 us; the launch traced here: 639 us
  waiting for transfers between devices  243 us (38%)
  starting transfers between devices  141 us (22%)
  local copies, waits for them, and re-layouts  108 us (17%)
  other arithmetic  62.5 us (10%)
  matrix products  49.7 us (8%)
  Pallas kernels  28.3 us (4%)
  between operations  7.01 us (1%)
    ppermute x16, waiting for transfers between devices, from_behind(): lax.ppermute(value, axis, [(source, source + steps) for source in range(l...  167 us
    ppermute x76, waiting for transfers between devices, swap(): return lax.ppermute(value, axis, [(i, i ^ 1 << bit) for i in range(count)])  76.4 us
    ppermute x16, starting transfers between devices, from_behind(): lax.ppermute(value, axis, [(source, source + steps) for source in range(l...  72.4 us
    ppermute x76, starting transfers between devices, swap(): return lax.ppermute(value, axis, [(i, i ^ 1 << bit) for i in range(count)])  68.2 us
    dot_general x24, matrix products, contract(): lax.dot_general(left, right, (((left_dim,), (right_dim,)), ((), ())), pre...  49.7 us
    unnamed x223, local copies, waits for them, and re-layouts  22.8 us
    pallas_call x2, Pallas kernels, attend_back(): pl.pallas_call(attend_back_kernel, grid_spec=pltpu.PrefetchScalarGridSpec...  15.9 us
    convert_element_type x29, other arithmetic, scatter_sum(): value = (kept.astype(F32) + swap(sent, axis, bit).astype(F32)).astype(BF16)  15.3 us
  transfers between devices with their start and end apart: 92, of which 42 were waited for; matrix products, arithmetic and copies ran while one was open for 23% of the time, Pallas kernels for 3%

profile of v3, /device:TPU:0, one launch (start us, length us, event | category | flops | bytes accessed | tf_op | source)
XLA Modules:
  0.0 639.2 jit_solution(10031480327241743351)
XLA Ops:
  48.2 6.9 %collective-permute-done.6 = bf16[384,512]{1,0:T(8,128)(2,1)S(1)} collective-permute-done((bf16[384,512]{1,0:T(8,128)(2,1)S(1)}, bf16[384,512]{1,0:T(8,128)(2,1)S(1)}, u32[]{:S(2)}, u32[]{:S(2)}) %collective-permute-start.6) | collective-permute-done | bytes 393248 | tf_op jit(solution)/shard_map/ppermute | solution.py:29
  55.6 7.4 %collective-permute-done.7 = bf16[384,512]{1,0:T(8,128)(2,1)S(1)} collective-permute-done((bf16[384,512]{1,0:T(8,128)(2,1)S(1)}, bf16[384,512]{1,0:T(8,128)(2,1)S(1)}, u32[]{:S(2)}, u32[]{:S(2)}) %collective-permute-start.7) | collective-permute-done | bytes 393248 | tf_op jit(solution)/shard_map/ppermute | solution.py:29
  63.2 6.2 shard_map.203
  70.8 5.0 collective-permute-done.12
  91.7 32.3 %collective-permute-start.21 = (bf16[384,512]{1,0:T(8,128)(2,1)S(1)}, bf16[384,512]{1,0:T(8,128)(2,1)S(1)}, u32[]{:S(2)}, u32[]{:S(2)}) collective-permute-start(bf16[384,512]{1,0:T(8,128)(2,1)S(1)} %pad_maximum_fusion.25), channel_id=1, source_target_pairs={{0,4},{1,5},{2,6},{3,7},{8,12},{9,13},{10,14},{11,15},{16,20},{17,... | collective-permute-start | bytes 1179656 | tf_op jit(solution)/shard_map/ppermute | solution.py:29
  123.9 11.1 %collective-permute-start.22 = (bf16[384,512]{1,0:T(8,128)(2,1)S(1)}, bf16[384,512]{1,0:T(8,128)(2,1)S(1)}, u32[]{:S(2)}, u32[]{:S(2)}) collective-permute-start(bf16[384,512]{1,0:T(8,128)(2,1)S(1)} %pad_maximum_fusion.25), channel_id=1, source_target_pairs={{0,3},{1,4},{2,5},{3,6},{4,7},{8,11},{9,12},{10,13},{11,14},{12,15... | collective-permute-start | bytes 1179656 | tf_op jit(solution)/shard_map/ppermute | solution.py:29
  145.6 6.5 %collective-permute-done.23 = bf16[384,512]{1,0:T(8,128)(2,1)S(1)} collective-permute-done((bf16[384,512]{1,0:T(8,128)(2,1)S(1)}, bf16[384,512]{1,0:T(8,128)(2,1)S(1)}, u32[]{:S(2)}, u32[]{:S(2)}) %collective-permute-start.23) | collective-permute-done | bytes 393248 | tf_op jit(solution)/shard_map/ppermute | solution.py:29
  152.2 6.2 shard_map.204
  159.8 6.2 collective-permute-done.28
  188.4 8.1 %shard_map.205 = (f32[576,512]{1,0:T(8,128)S(1)}, bf16[2,192,2560]{2,1,0:T(8,128)(2,1)S(1)}) custom-call(s32[1]{0:T(128)} %bitcast.9.first_ref, bf16[576,512]{1,0:T(8,128)(2,1)S(1)} %bitcast.414, bf16[576,512]{1,0:T(8,128)(2,1)S(1)} %copy-done.6, bf16[2,192,2560]{2,1,0:T(8,128)(2,1)S(1)} %bitcast.418, s32[3,512]{1,0:T(4,128)S(1)} %add_subtract_fusion.limits_ref, ...), custom_call_target="tpu_custom_call" | custom-call | flops 90596966400 | bytes 3932160 | tf_op jit(solution)/shard_map/pallas_call | solution.py:285
  203.6 4.8 reshape_reshape.45
  211.8 4.8 constant_dynamic-slice_fusion.27
  235.5 9.2 %collective-permute-done.41 = bf16[384,512]{1,0:T(8,128)(2,1)} collective-permute-done((bf16[384,512]{1,0:T(8,128)(2,1)}, bf16[384,512]{1,0:T(8,128)(2,1)}, u32[]{:S(2)}, u32[]{:S(2)}) %collective-permute-start.41) | collective-permute-done | bytes 393248 | tf_op jit(solution)/shard_map/ppermute | solution.py:29
  245.7 46.5 %collective-permute-done.42 = bf16[384,512]{1,0:T(8,128)(2,1)S(1)} collective-permute-done((bf16[384,512]{1,0:T(8,128)(2,1)S(1)}, bf16[384,512]{1,0:T(8,128)(2,1)S(1)}, u32[]{:S(2)}, u32[]{:S(2)}) %collective-permute-start.42) | collective-permute-done | bytes 393248 | tf_op jit(solution)/shard_map/ppermute | solution.py:29
  292.2 26.6 %collective-permute-done.43 = bf16[384,512]{1,0:T(8,128)(2,1)S(1)} collective-permute-done((bf16[384,512]{1,0:T(8,128)(2,1)S(1)}, bf16[384,512]{1,0:T(8,128)(2,1)S(1)}, u32[]{:S(2)}, u32[]{:S(2)}) %collective-permute-start.43) | collective-permute-done | bytes 393248 | tf_op jit(solution)/shard_map/ppermute | solution.py:29
  353.4 5.2 reshape_reshape.48
  358.6 7.6 %constant_dynamic-slice_fusion.18 = (bf16[2,1,384,576]{2,1,0,3:T(2,128)(2,1)}, bf16[2,1,384,576]{2,1,0,3:T(2,128)(2,1)}) fusion(bf16[2,2,384,576]{2,1,0,3:T(2,128)(2,1)} %reshape_reshape.48, s32[]{:T(128)S(6)} %select_n.442, s32[]{:T(128)S(6)} %select_n.443), kind=kLoop, calls=%fused_computation.302 | loop fusion | bytes 3538952 | tf_op jit(solution)/shard_map/jit(dynamic_index_in_dim)/dynamic_slice | solution.py:49
  379.5 7.7 %shard_map.206 = (f32[576,512]{1,0:T(8,128)S(1)}, bf16[2,192,2560]{2,1,0:T(8,128)(2,1)S(1)}) custom-call(s32[1]{0:T(128)} %bitcast.9.first_ref, bf16[576,512]{1,0:T(8,128)(2,1)S(1)} %bitcast.412, bf16[576,512]{1,0:T(8,128)(2,1)S(1)} %convolution_convert_fusion.8.grad_ref, bf16[2,192,2560]{2,1,0:T(8,128)(2,1)S(1)} %bitcast.416, ...), custom_call_target="tpu_custom_call" | custom-call | flops 90596966400 | bytes 3932160 | tf_op jit(solution)/shard_map/pallas_call | solution.py:285
  395.0 9.6 %collective-permute-start.86 = (bf16[4,432,128]{2,1,0:T(8,128)(2,1)S(1)}, bf16[4,432,128]{2,1,0:T(8,128)(2,1)S(1)}, u32[]{:S(2)}, u32[]{:S(2)}) collective-permute-start(bf16[4,432,128]{2,1,0:T(8,128)(2,1)S(1)} %copy-done.74), channel_id=1, source_target_pairs={{0,1},{1,0},{2,3},{3,2},{4,5},{5,4},{6,7},{7,6},{8,9},{9,8},{10,11... | collective-permute-start | bytes 1327112 | tf_op jit(solution)/shard_map/ppermute | solution.py:34
  408.4 17.7 %collective-permute-done.53 = bf16[384,512]{1,0:T(8,128)(2,1)S(1)} collective-permute-done((bf16[384,512]{1,0:T(8,128)(2,1)S(1)}, bf16[384,512]{1,0:T(8,128)(2,1)S(1)}, u32[]{:S(2)}, u32[]{:S(2)}) %collective-permute-start.53) | collective-permute-done | bytes 393248 | tf_op jit(solution)/shard_map/ppermute | solution.py:29
  426.2 8.5 %collective-permute-done.54 = bf16[384,512]{1,0:T(8,128)(2,1)S(1)} collective-permute-done((bf16[384,512]{1,0:T(8,128)(2,1)S(1)}, bf16[384,512]{1,0:T(8,128)(2,1)S(1)}, u32[]{:S(2)}, u32[]{:S(2)}) %collective-permute-start.54) | collective-permute-done | bytes 393248 | tf_op jit(solution)/shard_map/ppermute | solution.py:29
  434.7 32.9 %collective-permute-done.55 = bf16[384,512]{1,0:T(8,128)(2,1)S(1)} collective-permute-done((bf16[384,512]{1,0:T(8,128)(2,1)S(1)}, bf16[384,512]{1,0:T(8,128)(2,1)S(1)}, u32[]{:S(2)}, u32[]{:S(2)}) %collective-permute-start.55) | collective-permute-done | bytes 393248 | tf_op jit(solution)/shard_map/ppermute | solution.py:29
  527.2 6.7 %collective-permute-done.47 = bf16[1,144,3072]{2,1,0:T(8,128)(2,1)} collective-permute-done((bf16[1,144,3072]{2,1,0:T(8,128)(2,1)}, bf16[1,144,3072]{2,1,0:T(8,128)(2,1)}, u32[]{:S(2)}, u32[]{:S(2)}) %collective-permute-start.47) | collective-permute-done | bytes 884768 | tf_op jit(solution)/shard_map/ppermute | solution.py:34
  560.2 5.6 collective-permute-done.80
  (699 shorter events, 342.8 us)
Async XLA Ops:
  41.6 28.5 %collective-permute-start.15 = (bf16[384,576]{0,1:T(8,128)(2,1)S(1)}, bf16[384,576]{0,1:T(8,128)(2,1)S(1)}, u32[]{:S(2)}, u32[]{:S(2)}) collective-permute-start(bf16[384,576]{0,1:T(8,128)(2,1)S(1)} %get-tuple-element.42), channel_id=1, source_target_pairs={{0,16},{8,24},{16,0},{24,8},{1,17},{9,25},{17,1},{25,9},{2,18},{10... | collective-permute-start | bytes 1327112 | tf_op jit(solution)/shard_map/ppermute | solution.py:34
  48.0 27.7 %collective-permute-start.16 = (bf16[384,576]{0,1:T(8,128)(2,1)S(1)}, bf16[384,576]{0,1:T(8,128)(2,1)S(1)}, u32[]{:S(2)}, u32[]{:S(2)}) collective-permute-start(bf16[384,576]{0,1:T(8,128)(2,1)S(1)} %get-tuple-element.42), channel_id=1, source_target_pairs={{0,8},{8,0},{16,24},{24,16},{1,9},{9,1},{17,25},{25,17},{2,10},{10... | collective-permute-start | bytes 1327112 | tf_op jit(solution)/shard_map/ppermute | solution.py:34
  89.1 48.1 %collective-permute-start.25 = (bf16[144,576]{1,0:T(8,128)(2,1)S(1)}, bf16[144,576]{1,0:T(8,128)(2,1)S(1)}, u32[]{:S(2)}, u32[]{:S(2)}) collective-permute-start(bf16[144,576]{1,0:T(8,128)(2,1)S(1)} %get-tuple-element.45), channel_id=1, source_target_pairs={{0,16},{8,24},{16,0},{24,8},{1,17},{9,25},{17,1},{25,9},{2,18},{10... | collective-permute-start | bytes 497672 | tf_op jit(solution)/shard_map/ppermute | solution.py:34
  89.7 47.7 %collective-permute-start.26 = (bf16[144,576]{1,0:T(8,128)(2,1)S(1)}, bf16[144,576]{1,0:T(8,128)(2,1)S(1)}, u32[]{:S(2)}, u32[]{:S(2)}) collective-permute-start(bf16[144,576]{1,0:T(8,128)(2,1)S(1)} %get-tuple-element.45), channel_id=1, source_target_pairs={{0,8},{8,0},{16,24},{24,16},{1,9},{9,1},{17,25},{25,17},{2,10},{10... | collective-permute-start | bytes 497672 | tf_op jit(solution)/shard_map/ppermute | solution.py:34
  91.7 50.6 %collective-permute-start.21 = (bf16[384,512]{1,0:T(8,128)(2,1)S(1)}, bf16[384,512]{1,0:T(8,128)(2,1)S(1)}, u32[]{:S(2)}, u32[]{:S(2)}) collective-permute-start(bf16[384,512]{1,0:T(8,128)(2,1)S(1)} %pad_maximum_fusion.25), channel_id=1, source_target_pairs={{0,4},{1,5},{2,6},{3,7},{8,12},{9,13},{10,14},{11,15},{16,20},{17,... | collective-permute-start | bytes 1179656 | tf_op jit(solution)/shard_map/ppermute | solution.py:29
  135.1 24.1 %collective-permute-start.31 = (bf16[384,576]{0,1:T(8,128)(2,1)S(1)}, bf16[384,576]{0,1:T(8,128)(2,1)S(1)}, u32[]{:S(2)}, u32[]{:S(2)}) collective-permute-start(bf16[384,576]{0,1:T(8,128)(2,1)S(1)} %get-tuple-element.48), channel_id=1, source_target_pairs={{0,16},{8,24},{16,0},{24,8},{1,17},{9,25},{17,1},{25,9},{2,18},{10... | collective-permute-start | bytes 1327112 | tf_op jit(solution)/shard_map/ppermute | solution.py:34
  197.7 37.1 %collective-permute-start.40 = (bf16[384,512]{1,0:T(8,128)(2,1)}, bf16[384,512]{1,0:T(8,128)(2,1)}, u32[]{:S(2)}, u32[]{:S(2)}) collective-permute-start(bf16[384,512]{1,0:T(8,128)(2,1)} %get-tuple-element.127), channel_id=1, source_target_pairs={{1,0},{2,1},{3,2},{4,3},{5,4},{6,5},{7,6},{9,8},{10,9},{11,10},{12... | collective-permute-start | bytes 1179656 | tf_op jit(solution)/shard_map/ppermute | solution.py:29
  199.1 45.6 %collective-permute-start.41 = (bf16[384,512]{1,0:T(8,128)(2,1)}, bf16[384,512]{1,0:T(8,128)(2,1)}, u32[]{:S(2)}, u32[]{:S(2)}) collective-permute-start(bf16[384,512]{1,0:T(8,128)(2,1)} %get-tuple-element.130), channel_id=1, source_target_pairs={{2,0},{3,1},{4,2},{5,3},{6,4},{7,5},{10,8},{11,9},{12,10},{13,11},... | collective-permute-start | bytes 1179656 | tf_op jit(solution)/shard_map/ppermute | solution.py:29
  224.9 67.3 %collective-permute-start.42 = (bf16[384,512]{1,0:T(8,128)(2,1)S(1)}, bf16[384,512]{1,0:T(8,128)(2,1)S(1)}, u32[]{:S(2)}, u32[]{:S(2)}) collective-permute-start(bf16[384,512]{1,0:T(8,128)(2,1)S(1)} %copy-done.76), channel_id=1, source_target_pairs={{3,0},{4,1},{5,2},{6,3},{7,4},{11,8},{12,9},{13,10},{14,11},{15,12... | collective-permute-start | bytes 1179656 | tf_op jit(solution)/shard_map/ppermute | solution.py:29
  227.3 91.5 %collective-permute-start.43 = (bf16[384,512]{1,0:T(8,128)(2,1)S(1)}, bf16[384,512]{1,0:T(8,128)(2,1)S(1)}, u32[]{:S(2)}, u32[]{:S(2)}) collective-permute-start(bf16[384,512]{1,0:T(8,128)(2,1)S(1)} %copy-done.75), channel_id=1, source_target_pairs={{4,0},{5,1},{6,2},{7,3},{12,8},{13,9},{14,10},{15,11},{20,16},{21,... | collective-permute-start | bytes 1179656 | tf_op jit(solution)/shard_map/ppermute | solution.py:29
  233.3 88.4 %collective-permute-start.35 = (bf16[1,144,3072]{2,1,0:T(8,128)(2,1)S(1)}, bf16[1,144,3072]{2,1,0:T(8,128)(2,1)S(1)}, u32[]{:S(2)}, u32[]{:S(2)}) collective-permute-start(bf16[1,144,3072]{2,1,0:T(8,128)(2,1)S(1)} %constant_dynamic-slice_fusion.28), channel_id=1, source_target_pairs={{0,16},{8,24},{16,0},{24,8},{1,17},{9,25},{17,1},{25,9},{2,18},{10... | collective-permute-start | bytes 2654216 | tf_op jit(solution)/shard_map/ppermute | solution.py:34
  234.8 85.3 %collective-permute-start.39 = (bf16[1,144,576]{2,1,0:T(8,128)(2,1)S(1)}, bf16[1,144,576]{2,1,0:T(8,128)(2,1)S(1)}, u32[]{:S(2)}, u32[]{:S(2)}) collective-permute-start(bf16[1,144,576]{2,1,0:T(8,128)(2,1)S(1)} %constant_dynamic-slice_fusion.24), channel_id=1, source_target_pairs={{0,16},{8,24},{16,0},{24,8},{1,17},{9,25},{17,1},{25,9},{2,18},{10... | collective-permute-start | bytes 497672 | tf_op jit(solution)/shard_map/ppermute | solution.py:34
  244.7 76.2 %collective-permute-start.37 = (bf16[1,384,576]{1,2,0:T(8,128)(2,1)S(1)}, bf16[1,384,576]{1,2,0:T(8,128)(2,1)S(1)}, u32[]{:S(2)}, u32[]{:S(2)}) collective-permute-start(bf16[1,384,576]{1,2,0:T(8,128)(2,1)S(1)} %constant_dynamic-slice_fusion.25), channel_id=1, source_target_pairs={{0,16},{8,24},{16,0},{24,8},{1,17},{9,25},{17,1},{25,9},{2,18},{10... | collective-permute-start | bytes 1327112 | tf_op jit(solution)/shard_map/ppermute | solution.py:34
  343.9 26.4 %collective-permute-start.44 = (bf16[2,288]{1,0:T(2,128)(2,1)S(1)}, bf16[2,288]{1,0:T(2,128)(2,1)S(1)}, u32[]{:S(2)}, u32[]{:S(2)}) collective-permute-start(bf16[2,288]{1,0:T(2,128)(2,1)S(1)} %bitcast.485), channel_id=1, source_target_pairs={{0,8},{8,0},{16,24},{24,16},{1,9},{9,1},{17,25},{25,17},{2,10},{10... | collective-permute-start | bytes 3464 | tf_op jit(solution)/shard_map/ppermute | solution.py:34
  352.1 40.5 %collective-permute-start.56 = (bf16[4,304,128]{2,1,0:T(8,128)(2,1)}, bf16[4,304,128]{2,1,0:T(8,128)(2,1)}, u32[]{:S(2)}, u32[]{:S(2)}) collective-permute-start(bf16[4,304,128]{2,1,0:T(8,128)(2,1)} %dynamic-slice_bitcast_fusion.9), channel_id=1, source_target_pairs={{0,1},{1,0},{2,3},{3,2},{4,5},{5,4},{6,7},{7,6},{8,9},{9,8},{10,11... | collective-permute-start | bytes 933896 | tf_op jit(solution)/shard_map/ppermute | solution.py:34
  352.9 42.1 %collective-permute-start.50 = (bf16[2,144,576]{2,1,0:T(8,128)(2,1)}, bf16[2,144,576]{2,1,0:T(8,128)(2,1)}, u32[]{:S(2)}, u32[]{:S(2)}) collective-permute-start(bf16[2,144,576]{2,1,0:T(8,128)(2,1)} %dynamic-slice_bitcast_fusion.6), channel_id=1, source_target_pairs={{0,8},{8,0},{16,24},{24,16},{1,9},{9,1},{17,25},{25,17},{2,10},{10... | collective-permute-start | bytes 995336 | tf_op jit(solution)/shard_map/ppermute | solution.py:34
  388.9 37.2 %collective-permute-start.53 = (bf16[384,512]{1,0:T(8,128)(2,1)S(1)}, bf16[384,512]{1,0:T(8,128)(2,1)S(1)}, u32[]{:S(2)}, u32[]{:S(2)}) collective-permute-start(bf16[384,512]{1,0:T(8,128)(2,1)S(1)} %get-tuple-element.126), channel_id=1, source_target_pairs={{2,0},{3,1},{4,2},{5,3},{6,4},{7,5},{10,8},{11,9},{12,10},{13,11},... | collective-permute-start | bytes 1179656 | tf_op jit(solution)/shard_map/ppermute | solution.py:29
  390.2 44.4 %collective-permute-start.54 = (bf16[384,512]{1,0:T(8,128)(2,1)S(1)}, bf16[384,512]{1,0:T(8,128)(2,1)S(1)}, u32[]{:S(2)}, u32[]{:S(2)}) collective-permute-start(bf16[384,512]{1,0:T(8,128)(2,1)S(1)} %get-tuple-element.125), channel_id=1, source_target_pairs={{3,0},{4,1},{5,2},{6,3},{7,4},{11,8},{12,9},{13,10},{14,11},{15,12... | collective-permute-start | bytes 1179656 | tf_op jit(solution)/shard_map/ppermute | solution.py:29
  392.6 75.0 %collective-permute-start.55 = (bf16[384,512]{1,0:T(8,128)(2,1)S(1)}, bf16[384,512]{1,0:T(8,128)(2,1)S(1)}, u32[]{:S(2)}, u32[]{:S(2)}) collective-permute-start(bf16[384,512]{1,0:T(8,128)(2,1)S(1)} %get-tuple-element.124), channel_id=1, source_target_pairs={{4,0},{5,1},{6,2},{7,3},{12,8},{13,9},{14,10},{15,11},{20,16},{21,... | collective-permute-start | bytes 1179656 | tf_op jit(solution)/shard_map/ppermute | solution.py:29
  395.0 73.7 %collective-permute-start.86 = (bf16[4,432,128]{2,1,0:T(8,128)(2,1)S(1)}, bf16[4,432,128]{2,1,0:T(8,128)(2,1)S(1)}, u32[]{:S(2)}, u32[]{:S(2)}) collective-permute-start(bf16[4,432,128]{2,1,0:T(8,128)(2,1)S(1)} %copy-done.74), channel_id=1, source_target_pairs={{0,1},{1,0},{2,3},{3,2},{4,5},{5,4},{6,7},{7,6},{8,9},{9,8},{10,11... | collective-permute-start | bytes 1327112 | tf_op jit(solution)/shard_map/ppermute | solution.py:34
  408.4 94.3 %collective-permute-start.48 = (bf16[2,384,576]{1,2,0:T(8,128)(2,1)}, bf16[2,384,576]{1,2,0:T(8,128)(2,1)}, u32[]{:S(2)}, u32[]{:S(2)}) collective-permute-start(bf16[2,384,576]{1,2,0:T(8,128)(2,1)} %bitcast.403), channel_id=1, source_target_pairs={{0,8},{8,0},{16,24},{24,16},{1,9},{9,1},{17,25},{25,17},{2,10},{10... | collective-permute-start | bytes 2654216 | tf_op jit(solution)/shard_map/ppermute | solution.py:34
  426.1 89.3 %collective-permute-start.46 = (bf16[2,144,3072]{2,1,0:T(8,128)(2,1)}, bf16[2,144,3072]{2,1,0:T(8,128)(2,1)}, u32[]{:S(2)}, u32[]{:S(2)}) collective-permute-start(bf16[2,144,3072]{2,1,0:T(8,128)(2,1)} %dynamic-slice_bitcast_fusion), channel_id=1, source_target_pairs={{0,8},{8,0},{16,24},{24,16},{1,9},{9,1},{17,25},{25,17},{2,10},{10... | collective-permute-start | bytes 5308424 | tf_op jit(solution)/shard_map/ppermute | solution.py:34
  434.7 46.3 %collective-permute-start.62 = (bf16[2,144,960]{2,1,0:T(8,128)(2,1)S(1)}, bf16[2,144,960]{2,1,0:T(8,128)(2,1)S(1)}, u32[]{:S(2)}, u32[]{:S(2)}) collective-permute-start(bf16[2,144,960]{2,1,0:T(8,128)(2,1)S(1)} %copy-done.71), channel_id=1, source_target_pairs={{0,8},{8,0},{16,24},{24,16},{1,9},{9,1},{17,25},{25,17},{2,10},{10... | collective-permute-start | bytes 1658888 | tf_op jit(solution)/shard_map/ppermute | solution.py:34
  542.8 32.5 %collective-permute-start.64 = (bf16[2,144,960]{2,1,0:T(8,128)(2,1)}, bf16[2,144,960]{2,1,0:T(8,128)(2,1)}, u32[]{:S(2)}, u32[]{:S(2)}) collective-permute-start(bf16[2,144,960]{2,1,0:T(8,128)(2,1)} %dynamic-slice_bitcast_fusion.2), channel_id=1, source_target_pairs={{0,8},{8,0},{16,24},{24,16},{1,9},{9,1},{17,25},{25,17},{2,10},{10... | collective-permute-start | bytes 1658888 | tf_op jit(solution)/shard_map/ppermute | solution.py:34
  (174 other events, 1612.9 us)
